TPU v7x, 256 devices: a whole 4x4x8 slice. The times are simulated.
256 devices in a mesh: ctx: 64 (over y, z, core), head: 4 (over x).
Axes of the slice: x: 4, y: 4, z: 8, core: 2. Of those that a mesh axis runs over, the one named last changes fastest.
Arguments:
- queries: bfloat16 [8192, 32, 128], P('ctx', 'head'), may hold values from -70 to 70
- keys: bfloat16 [8192, 32, 128], P('ctx', 'head'), may hold values from -6 to 6
- values: bfloat16 [8192, 32, 128], P('ctx', 'head'), may hold values from -6 to 6
- teacher: bfloat16 [8192, 32, 128], P('ctx', 'head'), may hold values from -18 to 18
- wq: bfloat16 [32, 64, 128], P('head'), may hold values from -0.5 to 0.5
- wk: bfloat16 [32, 64, 128], P('head'), may hold values from -0.5 to 0.5
Outputs:
- student: bfloat16 [8192, 32, 128], P('ctx', 'head')
- loss: float32 [], replicated
- grad_wq: float32 [32, 64, 128], P('head')
- grad_wk: float32 [32, 64, 128], P('head')
All inputs are finite; a program needn't handle non-finite values.
Results may differ from a plain program's by a relative error of at most 0.006.
Values may be sent and summed in bfloat16 or wider, within the bound.
A program may use at most 128 MiB of HBM per device.

v0:
```python
import jax
import jax.numpy as jnp
from jax import lax
from jax.sharding import PartitionSpec as P

WIN = 64


def shifted(array, axis, by):
    length = lax.axis_size(axis)
    pairs = [(i, i + by) for i in range(length) if 0 <= i + by < length]
    return lax.ppermute(array, axis, pairs)


def carried_in(value, axis, join, neutral):
    count, mine = (lax.axis_size(axis), lax.axis_index(axis))
    pieces = jax.tree.map(lambda part: lax.all_gather(part, axis), value)
    subtotal = jax.tree.map(
        lambda part, zero: jnp.full_like(part, 0) + jnp.asarray(zero, part.dtype), value, neutral
    )

    def hop(position, subtotal):
        longer = join(subtotal, jax.tree.map(lambda part: part[position], pieces))
        return jax.tree.map(lambda new, old: jnp.where(position < mine, new, old), longer, subtotal)

    return lax.fori_loop(0, count - 1, hop, subtotal)


def carried_in_2(array, axis, combine, identity):
    length, index = (lax.axis_size(axis), lax.axis_index(axis))
    everything = jax.tree.map(
        lambda part, kind: lax.all_gather(part.astype(kind), axis),
        array,
        jax.tree.map(lambda a: jnp.bfloat16 if a.dtype == jnp.float32 else a.dtype, array),
    )
    start = jax.tree.map(
        lambda part, zero: jnp.broadcast_to(jnp.asarray(zero, part.dtype), part.shape),
        array,
        identity,
    )

    def hop(k, before):
        at = length - 1 - k
        reached = at > index
        new = combine(
            before, jax.tree.map(lambda part, own: part[at].astype(own.dtype), everything, array)
        )
        return jax.tree.map(lambda a, b: jnp.where(reached, a, b), new, before)

    return lax.fori_loop(0, length, hop, start)


def phi_parts(x, w):
    proj = jnp.einsum("thd,hfd->thf", x, w, preferred_element_type=jnp.float32)
    return (jax.nn.softmax(proj, axis=-1), jax.nn.softmax(-proj, axis=-1))


def phi_grad(x, parts, grad_feat):
    half = grad_feat.shape[-1] // 2
    up_part, down_part = parts
    g_up = grad_feat[..., :half]
    g_down = grad_feat[..., half:]
    d_proj = up_part * (g_up - jnp.sum(up_part * g_up, axis=-1, keepdims=True))
    d_proj = d_proj - down_part * (g_down - jnp.sum(down_part * g_down, axis=-1, keepdims=True))
    return jnp.einsum(
        "thf,thd->hfd", d_proj, x.astype(jnp.float32), precision=lax.Precision.HIGHEST
    )


def add_pair(earlier, later):
    return (earlier[0] + later[0], earlier[1] + later[1])


def per_device(queries, keys, values, teacher, wq, wk):
    high = lax.Precision.HIGHEST
    ntok, nhead, hdim = queries.shape
    width = WIN
    scale = 1.0 / hdim**0.5
    tail = jnp.stack([keys[ntok - width :], values[ntok - width :]])
    halo = shifted(tail, "ctx", 1)
    key_all = jnp.concatenate([halo[0], keys], axis=0)
    val_all = jnp.concatenate([halo[1], values], axis=0).astype(jnp.float32)
    first = lax.axis_index("ctx") * ntok
    pos = first - width + jnp.arange(width + ntok, dtype=jnp.int32)
    valid = (pos >= 0).astype(jnp.float32)
    early = first + jnp.arange(ntok, dtype=jnp.int32) < width
    rows = jnp.arange(ntok, dtype=jnp.int32)[:, None]
    cols = jnp.arange(width + ntok, dtype=jnp.int32)[None, :]
    inwin = (cols > rows) & (cols <= rows + width) & (pos[None, :] >= 0)
    lower = cols[:, :ntok] <= rows
    score = jnp.einsum("ihd,chd->hic", queries, key_all, preferred_element_type=jnp.float32) * scale
    score = jnp.where(inwin[None], score, -jnp.inf)
    top = jnp.max(score, axis=-1)
    weight = jnp.where(inwin[None], jnp.exp(score - top[..., None]), 0.0)
    win_num = jnp.einsum("hic,chd->ihd", weight, val_all, precision=high)
    win_den = jnp.sum(weight, axis=-1).T
    q_parts = phi_parts(queries, wq)
    fq = jnp.concatenate(q_parts, axis=-1)
    k_parts = phi_parts(key_all[:ntok], wk)
    fk = jnp.concatenate(k_parts, axis=-1) * valid[:ntok, None, None]
    val_own = val_all[:ntok]
    local_state = jnp.einsum("chf,chd->hfd", fk, val_own, precision=high)
    local_norm = jnp.sum(fk, axis=0)
    empty = (jnp.zeros_like(local_state), jnp.zeros_like(local_norm))
    state, norm = carried_in((local_state, local_norm), "ctx", add_pair, empty)
    amat = jnp.where(lower[None], jnp.einsum("ihf,chf->hic", fq, fk, precision=high), 0.0)
    lin_num = jnp.einsum("hic,chd->ihd", amat, val_own, precision=high) + jnp.einsum(
        "ihf,hfd->ihd", fq, state, precision=high
    )
    lin_den = jnp.sum(amat, axis=-1).T + jnp.einsum("ihf,hf->ih", fq, norm, precision=high)
    top_t = top.T
    win_scale = jnp.where(early[:, None], 1.0, jnp.exp(jnp.minimum(top_t, 0.0)))
    lin_scale = jnp.where(early[:, None], 0.0, jnp.exp(-jnp.maximum(top_t, 0.0)))
    denom = win_scale * win_den + lin_scale * lin_den
    out = (win_scale[..., None] * win_num + lin_scale[..., None] * lin_num) / denom[..., None]
    diff = out - teacher.astype(jnp.float32)
    grad_out = 2.0 * diff / hdim
    coef = lin_scale / denom
    grad_num = coef[..., None] * grad_out
    grad_den = -coef * jnp.sum(grad_out * out, axis=-1)
    mix = jnp.einsum("ihd,chd->hic", grad_num, val_own, precision=high) + grad_den.T[:, :, None]
    mix = jnp.where(lower[None], mix, 0.0)
    grad_fq = jnp.einsum("hic,chf->ihf", mix, fk, precision=high)
    grad_fq = (
        grad_fq
        + jnp.einsum("hfd,ihd->ihf", state, grad_num, precision=high)
        + norm[None] * grad_den[..., None]
    )
    later_state = jnp.einsum("ihf,ihd->hfd", fq, grad_num, precision=high)
    later_norm = jnp.einsum("ihf,ih->hf", fq, grad_den, precision=high)
    after_state, after_norm = carried_in_2((later_state, later_norm), "ctx", add_pair, empty)
    grad_fk = jnp.einsum("hic,ihf->chf", mix, fq, precision=high)
    grad_fk = (
        grad_fk
        + jnp.einsum("hfd,chd->chf", after_state, val_own, precision=high)
        + after_norm[None]
    )
    grad_fk = grad_fk * valid[:ntok, None, None]
    grad_q = phi_grad(queries, q_parts, grad_fq)
    grad_k = phi_grad(key_all[:ntok], k_parts, grad_fk)
    squared = jnp.sum(diff * diff)
    entries = ntok * lax.axis_size("ctx") * nhead * lax.axis_size("head") * hdim
    grad_q, grad_k = lax.psum((grad_q, grad_k), "ctx")
    total = lax.psum(squared, ("ctx", "head"))
    return (out.astype(jnp.bfloat16), total / entries, grad_q, grad_k)


def solution(mesh):
    placed = (
        P("ctx", "head", None),
        P("ctx", "head", None),
        P("ctx", "head", None),
        P("ctx", "head", None),
        P("head", None, None),
        P("head", None, None),
    )
    return jax.shard_map(
        per_device,
        mesh=mesh,
        in_specs=placed,
        out_specs=(P("ctx", "head", None), P(), P("head", None, None), P("head", None, None)),
        check_vma=False,
    )
```

profile of v0, /device:TPU:1, one launch (start us, length us, event | category | flops | bytes accessed | tf_op | source)
XLA Modules:
  0.0 669.2 jit_solution(3977496284294211692)
XLA Ops:
  9.3 4.9 collective-permute-start
  14.3 3.3 collective-permute-done
  17.6 1.3 fusion.95
  18.9 1.3 fusion.94
  23.0 1.2 fusion.96
  25.8 48.6 %all-gather.1 = f32[512,128]{1,0:T(8,128)S(1)} all-gather(f32[8,128]{1,0:T(8,128)S(1)} %fusion.57), channel_id=3, replica_groups=mesh['ctx'=64,'head'=4] {'ctx'}, dimensions={0}, use_global_device_ids=true | all-gather | bytes 266240 | tf_op jit(solution)/shard_map/all_gather | solution.py:17
  76.6 92.1 %all-gather.7.cloned.1.call-done = f32[512,128,128]{2,1,0:T(8,128)} async-done(((f32[8,128,128]{2,1,0:T(8,128)}), f32[512,128,128]{2,1,0:T(8,128)}) %all-gather.7.cloned.1.call-update) | async-done | bytes 33554448 | tf_op jit(solution)/shard_map/all_gather | solution.py:17
  168.7 80.1 %while.34 = (s32[]{:T(128)}, f32[8,128,128]{2,1,0:T(8,128)S(1)}, f32[8,128]{1,0:T(8,128)S(1)}, s32[]{:T(128)}, f32[64,8,128,128]{3,2,1,0:T(8,128)}, /*index=5*/f32[64,8,128]{2,1,0:T(8,128)S(1)}, s32[]{:T(128)}, s32[]{:T(128)}) while((s32[]{:T(128)}, f32[8,128,128]{2,1,0:T(8,128)S(1)}, f32[8,128]{1,0:T(8,128)S(1)}, s32[]{:T(128)}, ...), condition=%wide.region_11.12_spmd.clone, body=%wide.region_10.11_spmd.clone.sunk | while | flops 396292 | bytes 1585267 | solution.py:26
  251.0 3.4 multiply_reduce_fusion
  254.3 1.9 convolution_convert_fusion
  257.9 52.3 %all-gather.3 = bf16[512,128]{1,0:T(8,128)(2,1)} all-gather(bf16[8,128]{1,0:T(8,128)(2,1)S(1)} %convert_element_type.45), channel_id=5, replica_groups=mesh['ctx'=64,'head'=4] {'ctx'}, dimensions={0}, use_global_device_ids=true | all-gather | bytes 133120 | tf_op jit(solution)/shard_map/all_gather | solution.py:32
  312.2 1.3 convolution_bitcast_fusion.4
  316.6 36.1 %all-gather.9.cloned.1.call-done = bf16[512,128,128]{2,1,0:T(8,128)(2,1)} async-done(((bf16[8,128,128]{2,1,0:T(8,128)(2,1)}), bf16[512,128,128]{2,1,0:T(8,128)(2,1)}) %all-gather.9.cloned.1.call-update) | async-done | bytes 16777232 | tf_op jit(solution)/shard_map/all_gather | solution.py:32
  352.7 122.5 %while.35 = (s32[]{:T(128)}, f32[8,128,128]{2,1,0:T(8,128)S(1)}, f32[8,128]{1,0:T(8,128)S(1)}, s32[]{:T(128)}, bf16[64,8,128,128]{3,2,1,0:T(8,128)(2,1)}, /*inde...) while((s32[]{:T(128)}, f32[8,128,128]{2,1,0:T(8,128)S(1)}, ...), condition=%wide.region_21.22_spmd.clone, body=%wide.region_20.21_spmd.clone.sunk | while | flops 528392 | bytes 1321137 | solution.py:50
  352.7 1.2 add_select_fusion.10
  354.7 1.2 add_select_fusion.10
  356.6 1.2 add_select_fusion.10
  358.5 1.2 add_select_fusion.10
  360.4 1.2 add_select_fusion.10
  362.3 1.2 add_select_fusion.10
  364.3 1.2 add_select_fusion.10
  366.1 1.2 add_select_fusion.10
  368.1 1.2 add_select_fusion.10
  370.0 1.2 add_select_fusion.10
  371.9 1.2 add_select_fusion.10
  373.8 1.2 add_select_fusion.10
  375.7 1.2 add_select_fusion.10
  377.6 1.2 add_select_fusion.10
  379.6 1.2 add_select_fusion.10
  381.5 1.2 add_select_fusion.10
  383.4 1.2 add_select_fusion.10
  385.3 1.2 add_select_fusion.10
  387.2 1.2 add_select_fusion.10
  389.2 1.2 add_select_fusion.10
  391.1 1.2 add_select_fusion.10
  393.0 1.2 add_select_fusion.10
  394.9 1.2 add_select_fusion.10
  396.8 1.2 add_select_fusion.10
  398.7 1.2 add_select_fusion.10
  400.6 1.2 add_select_fusion.10
  402.5 1.2 add_select_fusion.10
  404.4 1.2 add_select_fusion.10
  406.4 1.2 add_select_fusion.10
  408.3 1.2 add_select_fusion.10
  410.2 1.2 add_select_fusion.10
  412.1 1.2 add_select_fusion.10
  414.0 1.2 add_select_fusion.10
  415.9 1.2 add_select_fusion.10
  417.9 1.2 add_select_fusion.10
  419.8 1.2 add_select_fusion.10
  421.7 1.2 add_select_fusion.10
  423.6 1.2 add_select_fusion.10
  425.5 1.2 add_select_fusion.10
  431.2 1.2 add_select_fusion.10
  454.2 1.2 add_select_fusion.10
  458.0 1.2 add_select_fusion.10
  473.4 1.2 add_select_fusion.10
  475.3 1.3 fusion.13
  477.8 2.0 fusion.36
  479.8 74.6 %psum.21 = f32[]{:T(128)} all-reduce(f32[]{:T(128)} %get-tuple-element.324), channel_id=1, replica_groups=mesh['ctx'=64,'head'=4] {'ctx','head'}, use_global_device_ids=true, to_apply=%region_15.16 | all-reduce | flops 1 | bytes 8 | tf_op jit(solution)/shard_map/psum | solution.py:144
  554.4 1.8 copy.51
  556.8 101.4 %all-reduce.3.cloned.1.call-done = (f32[8,64,128]{2,1,0:T(8,128)}, f32[8,64,128]{2,1,0:T(8,128)}) async-done(((f32[8,64,128]{2,1,0:T(8,128)}, f32[8,64,128]{2,1,0:T(8,128)}), (f32[8,64,128]{2,1,0:T(8,128)}, f32[8,64,128]{2,1,0:T(8,128)})) %all-reduce.3.cloned.1.call-update) | async-done | bytes 524304 | tf_op jit(solution)/shard_map/psum | solution.py:143
  658.2 1.7 copy.102
  659.9 1.7 copy.103
  (291 shorter events, 165.9 us)
Async XLA Ops:
  7.2 15.9 %copy-start = (bf16[128,8,128]{2,1,0:T(8,128)(2,1)S(1)}, bf16[128,8,128]{2,1,0:T(8,128)(2,1)}, u32[]{:S(2)}) copy-start(bf16[128,8,128]{2,1,0:T(8,128)(2,1)} %param.10) | copy-start | bytes 786436
  7.2 161.5 %all-gather.7.cloned.1.call-start = ((), (), s32[]{:S(2)}) async-start(), calls=%async_computation | async-start | bytes 34078720 | tf_op jit(solution)/shard_map/all_gather | solution.py:17
  9.2 65.6 %copy-start.1 = (bf16[128,8,128]{2,0,1:T(8,128)(2,1)}, bf16[128,8,128]{2,0,1:T(8,128)(2,1)S(1)}, u32[]{:S(2)}) copy-start(bf16[128,8,128]{2,0,1:T(8,128)(2,1)S(1)} %copy.31) | copy-start | bytes 786436
  9.3 8.2 %collective-permute-start = (bf16[2,64,8,128]{3,1,2,0:T(8,128)(2,1)S(1)}, bf16[2,64,8,128]{3,1,2,0:T(8,128)(2,1)S(1)}, u32[]{:S(2)}, u32[]{:S(2)}) collective-permute-start(bf16[2,64,8,128]{3,1,2,0:T(8,128)(2,1)S(1)} %pad_maximum_fusion.3), channel_id=1, source_target_pairs={{0,4},{4,8},{8,12},{12,16},{16,20},{20,24},{24,28},{28,32},{32,36}... | collective-permute-start | bytes 786440 | tf_op jit(solution)/shard_map/ppermute | solution.py:12
  14.3 236.1 %copy-start.15 = (f32[128]{0:T(128)}, f32[128]{0:T(128)S(1)}, u32[]{:S(2)}) copy-start(f32[128]{0:T(128)S(1)} %slice_convert_fusion) | copy-start | bytes 1540
  17.6 57.3 %copy-start.5 = (bf16[64,8,128]{2,0,1:T(8,128)(2,1)}, bf16[64,8,128]{2,0,1:T(8,128)(2,1)S(1)}, u32[]{:S(2)}) copy-start(bf16[64,8,128]{2,0,1:T(8,128)(2,1)S(1)} %get-tuple-element.361) | copy-start | bytes 393220
  18.8 1.4 copy-start.2
  18.9 2.7 copy-start.12
  20.2 1.3 copy-start.3
  20.2 1.3 copy-start.13
  21.5 331.2 %all-gather.9.cloned.1.call-start = ((), (), s32[]{:S(2)}) async-start(), calls=%async_computation.1 | async-start | bytes 17039360 | tf_op jit(solution)/shard_map/all_gather | solution.py:32
  22.8 228.0 %copy-start.16 = (pred[128]{0:T(512)(128)(4,1)}, pred[128]{0:T(512)(128)(4,1)S(1)}, u32[]{:S(2)}) copy-start(pred[128]{0:T(512)(128)(4,1)S(1)} %add_compare_fusion.1) | copy-start | bytes 388
  22.9 227.9 %copy-start.6 = (pred[128,128]{0,1:T(8,128)(4,1)}, pred[128,128]{0,1:T(8,128)(4,1)S(1)}, u32[]{:S(2)}) copy-start(pred[128,128]{0,1:T(8,128)(4,1)S(1)} %iota_compare_fusion.2) | copy-start | bytes 49156
  23.0 227.8 %copy-start.7 = (pred[128,192]{0,1:T(8,128)(4,1)}, pred[128,192]{0,1:T(8,128)(4,1)S(1)}, u32[]{:S(2)}) copy-start(pred[128,192]{0,1:T(8,128)(4,1)S(1)} %fusion.67) | copy-start | bytes 73732
  74.7 0.9 copy-start.4
  74.9 181.4 %copy-start.8 = (f32[8,128]{1,0:T(8,128)}, f32[8,128]{1,0:T(8,128)S(1)}, u32[]{:S(2)}) copy-start(f32[8,128]{1,0:T(8,128)S(1)} %fusion.25) | copy-start | bytes 12292
  76.6 174.2 %copy-start.9 = (f32[8,128]{1,0:T(8,128)}, f32[8,128]{1,0:T(8,128)S(1)}, u32[]{:S(2)}) copy-start(f32[8,128]{1,0:T(8,128)S(1)} %get-tuple-element.370) | copy-start | bytes 12292
  250.3 0.6 copy-start.10
  250.4 0.6 copy-start.11
  250.4 4.0 copy-start.14
  256.3 401.9 %all-reduce.3.cloned.1.call-start = ((), (), s32[]{:S(2)}) async-start(), calls=%async_computation.2 | async-start | bytes 1048576 | tf_op jit(solution)/shard_map/psum | solution.py:143
Sparse Core Ops, SparseCore 0:
  21.6 147.0 all-gather.6
  256.4 96.3 all-gather.8
  479.9 178.2 all-reduce.2
where the time goes:
time: 678 us; the launch traced here: 669 us
  waiting for transfers between devices  233 us (34%)
  other arithmetic  204 us (30%)
  blocking collectives  175 us (26%)
  matrix products  24.6 us (4%)
  between operations  16 us (2%)
  local copies, waits for them, and re-layouts  9.21 us (1%)
    select_n x128, other arithmetic, hop(): return jax.tree.map(lambda a, b: jnp.where(reached, a, b), new, before)  122 us
    psum x1, waiting for transfers between devices, per_device(): grad_q, grad_k = lax.psum((grad_q, grad_k), 'ctx')  101 us
    all_gather x1, waiting for transfers between devices, carried_in(): pieces = jax.tree.map(lambda part: lax.all_gather(part, axis), value)  92.1 us
    select_n x126, other arithmetic, hop(): jnp.where(position < mine, new, old)  78 us
    psum x1, blocking collectives, per_device(): total = lax.psum(squared, ('ctx', 'head'))  74.6 us
    all_gather x1, blocking collectives, carried_in_2(): lax.all_gather(part.astype(kind), axis)  52.3 us
    all_gather x1, blocking collectives, carried_in(): pieces = jax.tree.map(lambda part: lax.all_gather(part, axis), value)  48.6 us
    all_gather x1, waiting for transfers between devices, carried_in_2(): lax.all_gather(part.astype(kind), axis)  36.1 us
  transfers between devices with their start and end apart: 4, of which 4 were waited for; matrix products, arithmetic and copies ran while one was open for 2% of the time, Pallas kernels for 0%

commit v1 on v0

v1 whole, which is shorter than its diff:
```python
import jax
import jax.numpy as jnp
from jax import lax
from jax.experimental import pallas as pl
from jax.experimental.pallas import tpu as pltpu
from jax.sharding import PartitionSpec as P

NB = 8
CH = 128
WIN = 64
HD = 128
HF = 64
AUG = 144
FAR = (4, 3, 5, 2, 6, 1, 7, 0)
MESH = pl.DeviceIdType.MESH
BF = jnp.bfloat16
F32 = jnp.float32


def nt(a, b):
    return lax.dot_general(a, b, (((1,), (1,)), ((), ())), preferred_element_type=F32)


def nn(a, b):
    return jnp.dot(a, b, preferred_element_type=F32)


def halves(proj):
    e = []
    for s in (proj[:HF], proj[HF:]):
        w = jnp.exp(s - jnp.max(s, axis=0, keepdims=True))
        e.append(w * (1.0 / jnp.sum(w, axis=0, keepdims=True)))
    return jnp.concatenate(e, axis=0)


def proj_grad(feat, grad):
    d = []
    for a in (0, HF):
        u, g = feat[a : a + HF], grad[a : a + HF]
        d.append(u * (g - jnp.sum(u * g, axis=0, keepdims=True)))
    return (d[0] - d[1]).astype(BF)


def split(x):
    norm = x[HD : HD + 1]
    high = norm.astype(BF).astype(F32)
    row = lax.broadcasted_iota(jnp.int32, (AUG - HD, CH), 0)
    aug = jnp.where(row == 0, high, jnp.where(row == 1, norm - high, 0.0))
    return jnp.concatenate([x[:HD], aug], axis=0).astype(BF)


def joined(x):
    return jnp.concatenate([x[:HD], x[HD : HD + 8] + pltpu.roll(x[HD : HD + 8], 7, 0), x[HD + 8 :]], axis=0)


def place(block, head):
    return 16 * (block // 2) + 2 * head + lax.rem(block, 2)


def each(body):
    for n in range(NB):
        body(n)


def kernel(
    q_in, k_in, v_in, t_in, wq_ref, wk_ref,
    stu_out, gq_out, gk_out, loss_out,
    kbuf, vbuf, qbuf, tbuf, fkt, fkb, fqt, fqb, vta, pre, tot, win, lin, gna, gfk, later,
    own1, ag1, own2, ag2, stu, rs_own, rs_got, fin, la, lb, lc, scal,
    x_send, x_recv, h_send, h_recv, a1_send, a1_recv, a2_send, a2_recv,
    s_send, s_recv, r_send, r_recv, f_send, f_recv, l_send, l_recv,
):
    me = lax.axis_index("ctx")
    xme = lax.axis_index("head")
    src_b, src_j = me // NB, lax.rem(me, NB)
    b = 2 * (me // 16) + lax.rem(me, 2)
    h = lax.rem(me, 16) // 2
    first_block = b == 0

    def ctx(i):
        return {"ctx": i}

    bar = pltpu.get_barrier_semaphore()

    def greet(o, _):
        pl.semaphore_signal(bar, inc=1, device_id=ctx(lax.rem(me + o, 64)), device_id_type=MESH)
        return 0

    lax.fori_loop(1, 64, greet, 0)
    for o in range(1, 4):
        pl.semaphore_signal(bar, inc=1, device_id={"head": lax.rem(xme + o, 4)}, device_id_type=MESH)
    pl.semaphore_wait(bar, 66)

    arrays = ((k_in, kbuf, WIN), (v_in, vbuf, WIN), (q_in, qbuf, 0), (t_in, tbuf, 0))

    def exchange(a, o, act):
        src, dst, base = arrays[a]
        hd = lax.rem(h + o, NB)
        to = place(src_b, hd)
        rows = dst.at[pl.ds(pl.multiple_of(base + CH * src_j, WIN), CH)]

        def remote():
            act(pltpu.make_async_remote_copy(
                src.at[hd], rows, x_send.at[a, o], x_recv.at[a], device_id=ctx(to), device_id_type=MESH))

        if o == 0:
            pl.when(to != me)(remote)
            if act is go:
                @pl.when(to == me)
                def _():
                    pltpu.make_async_copy(src.at[hd], rows, x_recv.at[a]).start()
        else:
            remote()

    def go(c):
        c.start()

    def sent(c):
        c.wait_send()

    tail = jnp.logical_and(src_j == NB - 1, src_b < NB - 1)

    def halo(a, o, act):
        src, dst, _ = arrays[a]
        hd = lax.rem(h + o, NB)
        to = place(src_b + 1, hd)

        def remote():
            act(pltpu.make_async_remote_copy(
                src.at[hd, pl.ds(CH - WIN, WIN)], dst.at[pl.ds(0, WIN)], h_send.at[a, o], h_recv.at[a],
                device_id=ctx(to), device_id_type=MESH))

        if o == 0:
            pl.when(to != me)(remote)
            if act is go:
                @pl.when(to == me)
                def _():
                    pltpu.make_async_copy(
                        src.at[hd, pl.ds(CH - WIN, WIN)], dst.at[pl.ds(0, WIN)], h_recv.at[a]).start()
        else:
            remote()

    for o in FAR:
        exchange(0, o, go)
        exchange(1, o, go)

    @pl.when(tail)
    def _():
        for o in FAR:
            halo(0, o, go)
            halo(1, o, go)

    for a in (2, 3):
        for o in FAR:
            exchange(a, o, go)

    @pl.when(first_block)
    def _():
        kbuf[pl.ds(0, WIN)] = jnp.zeros((WIN, HD), BF)
        vbuf[pl.ds(0, WIN)] = jnp.zeros((WIN, HD), BF)

    eye = jnp.where(
        lax.broadcasted_iota(jnp.int32, (CH, CH), 0) == lax.broadcasted_iota(jnp.int32, (CH, CH), 1),
        1.0, 0.0).astype(BF)
    one_row = jnp.where(lax.broadcasted_iota(jnp.int32, (AUG - HD, CH), 0) < 2, 1.0, 0.0)
    wq1, wk1 = wq_ref[h], wk_ref[h]
    w2q = jnp.concatenate([wq1, -wq1], axis=0)
    w2k = jnp.concatenate([wk1, -wk1], axis=0)

    def arrived(a):
        src, dst, base = arrays[a]
        part = dst.at[pl.ds(base, NB * CH)]
        pltpu.make_async_copy(part, part, x_recv.at[a]).wait()

    def halo_arrived(a):
        dst = arrays[a][1]
        part = dst.at[pl.ds(0, WIN)]
        pltpu.make_async_copy(part, part, h_recv.at[a]).wait()

    arrived(0)
    arrived(1)

    @pl.when(b > 0)
    def _():
        halo_arrived(0)
        halo_arrived(1)

    cidx = lax.broadcasted_iota(jnp.int32, (CH, CH), 0)
    iidx = lax.broadcasted_iota(jnp.int32, (CH, CH), 1)
    lower = cidx <= iidx

    tot[...] = jnp.zeros((AUG, CH), F32)

    def key_chunk(n):
        f = halves(nt(w2k, kbuf[pl.ds(n * CH, CH)]))
        if n == 0:
            bad = jnp.logical_and(first_block, iidx < WIN)
            f = jnp.where(bad, 0.0, f)
        fkt[n] = f
        fb = f.astype(BF)
        fk = nt(eye, fb).astype(BF)
        fkb[n] = fk
        va = jnp.concatenate([nt(eye, vbuf[pl.ds(n * CH, CH)]), one_row], axis=0).astype(BF)
        vta[n] = va
        pre[n] = tot[...]
        tot[...] += nn(va, fk)

    each(key_chunk)
    vta[NB, :, pl.ds(0, WIN)] = jnp.concatenate(
        [nt(eye, vbuf[pl.ds(NB * CH, WIN)]), one_row[:, :WIN]], axis=0).astype(BF)
    own1[...] = split(tot[...])

    def scan_copy(o, own, got, send, recv):
        return pltpu.make_async_remote_copy(
            own, got.at[b], send.at[o], recv.at[b], device_id=ctx(place(lax.rem(b + o, NB), h)),
            device_id_type=MESH)

    def forward(o, act):
        @pl.when(b + o < NB)
        def _():
            act(scan_copy(o, own1, ag1, a1_send, a1_recv))

    def backward(o, act):
        @pl.when(b - o >= 0)
        def _():
            act(scan_copy(NB - o, own2, ag2, a2_send, a2_recv))

    for o in range(7, 0, -1):
        forward(o, go)

    arrived(2)
    scale = 1.0 / HD**0.5

    def query_chunk(n):
        q = qbuf[pl.ds(n * CH, CH)]
        f = halves(nt(w2q, q))
        fqt[n] = f
        fb = f.astype(BF)
        fqb[n] = fb
        sc = nt(kbuf[pl.ds(n * CH, CH + WIN)], q) * scale
        ci = lax.broadcasted_iota(jnp.int32, (CH + WIN, CH), 0)
        ii = lax.broadcasted_iota(jnp.int32, (CH + WIN, CH), 1)
        inwin = jnp.logical_and(ci > ii, ci <= ii + WIN)
        if n == 0:
            inwin = jnp.logical_and(inwin, jnp.logical_or(ci >= WIN, b > 0))
        sc = jnp.where(inwin, sc, -jnp.inf)
        top = jnp.max(sc, axis=0, keepdims=True)
        w = jnp.exp(sc - top).astype(BF)
        wn = nn(vta[n], w[:CH]) + nn(vta[n + 1, :, pl.ds(0, WIN)], w[CH:])
        ws = jnp.exp(jnp.minimum(top, 0.0))
        ls = jnp.exp(-jnp.maximum(top, 0.0))
        if n == 0:
            early = jnp.logical_and(first_block, lax.broadcasted_iota(jnp.int32, (1, CH), 1) < WIN)
            ws = jnp.where(early, 1.0, ws)
            ls = jnp.where(early, 0.0, ls)
        am = jnp.where(lower, nn(fkb[n], fb), 0.0).astype(BF)
        ln = nn(vta[n], am) + nn(split(pre[n]), fb)
        win[n] = ws * wn + ls * ln
        scal[n] = jnp.broadcast_to(ls, (8, CH))

    each(query_chunk)

    lin[...] = jnp.zeros((AUG, CH), F32)
    for m in range(NB - 1):
        @pl.when(m < b)
        def _():
            pltpu.make_async_copy(ag1.at[m], ag1.at[m], a1_recv.at[m]).wait()
            lin[...] += ag1[m].astype(F32)
    carry = joined(lin[...])
    carry_b = split(carry)
    arrived(3)

    la[b] = jnp.zeros((8, CH), F32)
    later[NB - 1] = jnp.zeros((AUG, CH), F32)

    def out_chunk(k):
        n = NB - 1 - k
        ls = scal[n][:1]
        full = win[n] + ls * nn(carry_b, fqb[n])
        inv = 1.0 / full[HD : HD + 1]
        out = full[:HD] * inv
        stu[n] = nt(eye, out.astype(BF)).astype(BF)
        diff = out - nt(eye, tbuf[pl.ds(n * CH, CH)])
        sq = diff * diff
        acc = sq[0:8]
        for r in range(1, HD // 8):
            acc = acc + sq[8 * r : 8 * r + 8]
        la[b] += acc
        coef = ls * inv
        g = diff * (2.0 / HD)
        gd = -coef * jnp.sum(g * out, axis=0, keepdims=True)
        scal[n] = jnp.broadcast_to(gd, (8, CH))
        ga = jnp.concatenate([coef * g, gd * one_row], axis=0).astype(BF)
        gna[n] = ga
        step = nt(ga, fqb[n])
        if n > 0:
            later[n - 1] = later[n] + step
        else:
            own2[...] = split(later[0] + step)

    each(out_chunk)
    for o in range(7, 0, -1):
        backward(o, go)

    def student(j, act):
        to = NB * b + j

        def remote():
            act(pltpu.make_async_remote_copy(
                stu.at[j], stu_out.at[h], s_send.at[j], s_recv, device_id=ctx(to), device_id_type=MESH))

        pl.when(to != me)(remote)
        if act is go:
            @pl.when(to == me)
            def _():
                pltpu.make_async_copy(stu.at[j], stu_out.at[h], s_recv).start()

    for j in range(NB):
        student(j, go)

    def loss_a(o, act):
        act(pltpu.make_async_remote_copy(
            la.at[b], la.at[b], l_send.at[0, o], l_recv.at[0],
            device_id=ctx(place(lax.rem(b + o, NB), h)), device_id_type=MESH))

    def loss_b(o, act):
        act(pltpu.make_async_remote_copy(
            lb.at[xme], lb.at[xme], l_send.at[1, o], l_recv.at[1],
            device_id={"head": lax.rem(xme + o, 4)}, device_id_type=MESH))

    def loss_c(o, act):
        act(pltpu.make_async_remote_copy(
            lc.at[h], lc.at[h], l_send.at[2, o], l_recv.at[2],
            device_id=ctx(place(b, lax.rem(h + o, NB))), device_id_type=MESH))

    def total(ref, count, level):
        part = ref.at[pl.ds(0, count - 1)]
        pltpu.make_async_copy(part, part, l_recv.at[level]).wait()
        acc = ref[0]
        for m in range(1, count):
            acc = acc + ref[m]
        return acc

    for o in range(1, NB):
        loss_a(o, go)

    dq = []

    def mix_chunk(n):
        gd = scal[n][:1]
        ga = gna[n]
        mx = nn(vbuf[pl.ds(n * CH, CH)], ga[:HD]) + gd
        mx = jnp.where(lower, mx, 0.0).astype(BF)
        st = nt(eye, split(pre[n] + carry)).astype(BF)
        gq = nn(fkt[n].astype(BF), mx) + nn(st, ga)
        dq.append(proj_grad(fqt[n], gq))
        lt = nt(eye, split(later[n])).astype(BF)
        gfk[n] = nt(fqb[n], mx) + nn(lt, vta[n])

    each(mix_chunk)
    grad_q = nn(jnp.concatenate(dq, axis=1), qbuf[...])
    rs_own[pl.ds(0, HF)] = grad_q.astype(BF)

    lb[xme] = total(la, NB, 0)
    for o in range(1, 4):
        loss_b(o, go)

    lin[...] = jnp.zeros((AUG, CH), F32)
    for m in range(1, NB):
        @pl.when(m > b)
        def _():
            pltpu.make_async_copy(ag2.at[m], ag2.at[m], a2_recv.at[m]).wait()
            lin[...] += ag2[m].astype(F32)
    after = nt(eye, split(joined(lin[...]))).astype(BF)
    dk = []

    def key_grad(n):
        dk.append(proj_grad(fkt[n], gfk[n] + nn(after, vta[n])))

    each(key_grad)
    grad_k = nn(jnp.concatenate(dk, axis=1), kbuf[pl.ds(0, NB * CH)])
    rs_own[pl.ds(HF, HF)] = grad_k.astype(BF)

    def reduce(o, act):
        m = lax.rem(b + o, NB)
        act(pltpu.make_async_remote_copy(
            rs_own.at[pl.ds(pl.multiple_of(16 * m, 16), 16)], rs_got.at[b], r_send.at[o], r_recv,
            device_id=ctx(place(m, h)), device_id_type=MESH))

    for o in range(1, NB):
        reduce(o, go)
    rs_got[b] = rs_own[pl.ds(pl.multiple_of(16 * b, 16), 16)]
    lc[h] = total(lb, 4, 1)
    for o in range(1, NB):
        loss_c(o, go)
    part = rs_got.at[pl.ds(0, NB - 1)]
    pltpu.make_async_copy(part, part, r_recv).wait()
    acc = rs_got[0].astype(F32)
    for m in range(1, NB):
        acc = acc + rs_got[m].astype(F32)
    slot = NB * h + b
    fin[slot] = acc.astype(BF)

    def spread(o, _):
        pltpu.make_async_remote_copy(
            fin.at[slot], fin.at[slot], f_send, f_recv,
            device_id=ctx(lax.rem(me + o, 64)), device_id_type=MESH).start()
        return 0

    lax.fori_loop(1, 64, spread, 0)

    loss_out[...] = total(lc, NB, 2)

    for o in range(NB):
        for a in range(4):
            exchange(a, o, sent)

    @pl.when(tail)
    def _():
        for o in range(NB):
            halo(0, o, sent)
            halo(1, o, sent)

    for o in range(1, NB):
        forward(o, sent)
        backward(o, sent)
        loss_a(o, sent)
        loss_c(o, sent)
        reduce(o, sent)
    for o in range(1, 4):
        loss_b(o, sent)
    for j in range(NB):
        student(j, sent)
    pltpu.make_async_copy(stu_out, stu_out, s_recv).wait()
    part = fin.at[pl.ds(0, 63)]
    pltpu.make_async_copy(part, part, f_send).wait()
    pltpu.make_async_copy(part, part, f_recv).wait()
    for d in range(NB):
        for m in range(4):
            gq_out[d, pl.ds(16 * m, 16)] = fin[NB * d + m].astype(F32)
            gk_out[d, pl.ds(16 * m, 16)] = fin[NB * d + 4 + m].astype(F32)


def per_device(queries, keys, values, teacher, wq, wk):
    heads = [jnp.swapaxes(x, 0, 1) for x in (queries, keys, values, teacher)]
    vm = pl.BlockSpec(memory_space=pltpu.VMEM)
    hbm = pl.BlockSpec(memory_space=pl.ANY)
    dma = pltpu.SemaphoreType.DMA
    stu, gq, gk, loss = pl.pallas_call(
        kernel,
        out_shape=(
            jax.ShapeDtypeStruct((NB, CH, HD), BF),
            jax.ShapeDtypeStruct((NB, HF, HD), F32),
            jax.ShapeDtypeStruct((NB, HF, HD), F32),
            jax.ShapeDtypeStruct((8, CH), F32),
        ),
        in_specs=[hbm] * 4 + [vm] * 2,
        out_specs=(vm, vm, vm, vm),
        scratch_shapes=[
            pltpu.VMEM((NB * CH + WIN, HD), BF),
            pltpu.VMEM((NB * CH + WIN, HD), BF),
            pltpu.VMEM((NB * CH, HD), BF),
            pltpu.VMEM((NB * CH, HD), BF),
            pltpu.VMEM((NB, CH, CH), F32),
            pltpu.VMEM((NB, CH, CH), BF),
            pltpu.VMEM((NB, CH, CH), F32),
            pltpu.VMEM((NB, CH, CH), BF),
            pltpu.VMEM((NB + 1, AUG, CH), BF),
            pltpu.VMEM((NB, AUG, CH), F32),
            pltpu.VMEM((AUG, CH), F32),
            pltpu.VMEM((NB, AUG, CH), F32),
            pltpu.VMEM((AUG, CH), F32),
            pltpu.VMEM((NB, AUG, CH), BF),
            pltpu.VMEM((NB, CH, CH), F32),
            pltpu.VMEM((NB, AUG, CH), F32),
            pltpu.VMEM((AUG, CH), BF),
            pltpu.VMEM((NB, AUG, CH), BF),
            pltpu.VMEM((AUG, CH), BF),
            pltpu.VMEM((NB, AUG, CH), BF),
            pltpu.VMEM((NB, CH, HD), BF),
            pltpu.VMEM((2 * HF, HD), BF),
            pltpu.VMEM((NB, 16, HD), BF),
            pltpu.VMEM((NB * NB, 16, HD), BF),
            pltpu.VMEM((NB, 8, CH), F32),
            pltpu.VMEM((4, 8, CH), F32),
            pltpu.VMEM((NB, 8, CH), F32),
            pltpu.VMEM((NB, 8, CH), F32),
            dma((4, NB)), dma((4,)),
            dma((2, NB)), dma((2,)),
            dma((NB,)), dma((NB,)),
            dma((NB,)), dma((NB,)),
            dma((NB,)), dma,
            dma((NB,)), dma,
            dma, dma,
            dma((3, NB)), dma((3,)),
        ],
        compiler_params=pltpu.CompilerParams(collective_id=0, has_side_effects=True),
    )(*heads, wq, wk)
    entries = 8192 * 32 * 128
    return jnp.swapaxes(stu, 0, 1), jnp.sum(loss) / entries, gq, gk


def solution(mesh):
    tok = P("ctx", "head", None)
    par = P("head", None, None)
    return jax.shard_map(
        per_device,
        mesh=mesh,
        in_specs=(tok, tok, tok, tok, par, par),
        out_specs=(tok, P(), par, par),
        check_vma=False,
    )
```

time: 678 us -> 70.7 us (0.10); the launches traced: 669 us -> 70.5 us
  waiting for transfers between devices: 233 us -> 0 us
  other arithmetic: 204 us -> 0.6 us
  blocking collectives: 175 us -> 0 us
  Pallas kernels: 0 us -> 60.3 us
  matrix products: 24.6 us -> 0 us
  between operations: 16 us -> 2.46 us
    select_n x254 -> x0, other arithmetic: 200 us -> none  [the longest x128 122 us: hop(): return jax.tree.map(lambda a, b: jnp.where(reached, a, b), new, before)]
    all_gather x2 -> x0, waiting for transfers between devices: 128 us -> none  [the longest x1 92.1 us: carried_in(): pieces = jax.tree.map(lambda part: lax.all_gather(part, axis), value)]
    psum x1 -> x0, waiting for transfers between devices: 101 us -> none  [per_device(): grad_q, grad_k = lax.psum((grad_q, grad_k), 'ctx')]
    all_gather x2 -> x0, blocking collectives: 101 us -> none  [the longest x1 52.3 us: carried_in_2(): lax.all_gather(part.astype(kind), axis)]
    psum x1 -> x0, blocking collectives: 74.6 us -> none  [per_device(): total = lax.psum(squared, ('ctx', 'head'))]
    pallas_call x0 -> x1, Pallas kernels: none -> 60.3 us  [per_device(): pl.pallas_call(kernel, out_shape=(jax.ShapeDtypeStruct((NB, CH, HD), BF),...]
    dot_general x16 -> x0, matrix products: 19.6 us -> none  [the longest x1 3.39 us: per_device(): win_num = jnp.einsum('hic,chd->ihd', weight, val_all, precision=high)]
  transfers between devices with their start and end apart: 4 -> 0, of which waited for: 4 -> 0; matrix products, arithmetic and copies ran while one was open for 2% -> 0% of each run, Pallas kernels for 0% -> 0%
where the time goes in v1:
time: 70.7 us; the launch traced here: 70.5 us
  Pallas kernels  60.3 us (85%)
  local copies, waits for them, and re-layouts  7.15 us (10%)
  between operations  2.46 us (3%)
    pallas_call x1, Pallas kernels, per_device(): pl.pallas_call(kernel, out_shape=(jax.ShapeDtypeStruct((NB, CH, HD), BF),...  60.3 us
    unnamed x13, local copies, waits for them, and re-layouts  4.29 us
    transpose x2, local copies, waits for them, and re-layouts, per_device(): heads = [jnp.swapaxes(x, 0, 1) for x in (queries, keys, values, teacher)]  2.85 us

profile of v1, /device:TPU:1, one launch (start us, length us, event | category | flops | bytes accessed | tf_op | source)
XLA Modules:
  0.0 70.5 jit_solution(16938396649354000514)
XLA Ops:
  0.6 0.0 copy-start.2
  0.6 0.0 copy-start.3
  0.7 2.0 %copy_bitcast_fusion.2 = (bf16[8,128,128]{2,1,0:T(8,128)(2,1)}, bf16[8,128,128]{2,1,0:T(8,128)(2,1)}) fusion(bf16[128,8,128]{2,1,0:T(8,128)(2,1)} %param.7, bf16[128,8,128]{2,1,0:T(8,128)(2,1)} %param.6), kind=kLoop, calls=%fused_computation.2 | loop fusion | bytes 1048576 | tf_op jit(solution)/shard_map/transpose | solution.py:445
  2.6 0.0 copy-done.2
  2.6 0.0 copy-done.3
  2.6 0.9 %copy_bitcast_fusion = (bf16[8,128,128]{2,1,0:T(8,128)(2,1)}, bf16[8,128,128]{2,1,0:T(8,128)(2,1)}) fusion(bf16[128,8,128]{2,1,0:T(8,128)(2,1)S(1)} %copy-done.2, bf16[128,8,128]{2,1,0:T(8,128)(2,1)S(1)} %copy-done.3), kind=kLoop, calls=%fused_computation | loop fusion | bytes 1048576 | tf_op jit(solution)/shard_map/transpose | solution.py:445
  3.5 60.3 %shard_map.93 = (bf16[8,128,128]{2,1,0:T(8,128)(2,1)}, f32[8,64,128]{2,1,0:T(8,128)}, f32[8,64,128]{2,1,0:T(8,128)}, f32[8,128]{1,0:T(8,128)}) custom-call(bf16[8,128,128]{2,1,0:T(8,128)(2,1)} %get-tuple-element.19.q_in, bf16[8,128,128]{2,1,0:T(8,128)(2,1)} %get-tuple-element.18.k_in, bf16[8,128,128]{2,1,0:T(8,128)(2,1)} %get-tuple-element.17.v_in, ...), custom_call_target="tpu_custom_call" | custom-call | tf_op jit(solution)/shard_map/pallas_call | solution.py:449
  63.8 0.0 copy-start.4
  63.8 0.7 copy-done.4
  64.5 0.6 reduce_sum.9
  65.7 0.0 copy-start.1
  65.7 1.9 %copy.14 = bf16[128,8,128]{2,1,0:T(8,128)(2,1)} copy(bf16[128,8,128]{2,0,1:T(8,128)(2,1)} %bitcast.9) | data formatting | bytes 524288
  67.6 0.0 copy-done.1
  67.6 0.0 copy-start
  67.6 0.7 copy.21
  68.3 0.3 copy-done
  68.6 0.7 copy.22
Async XLA Ops:
  0.6 2.0 %copy-start.2 = (bf16[128,8,128]{2,1,0:T(8,128)(2,1)S(1)}, bf16[128,8,128]{2,1,0:T(8,128)(2,1)}, u32[]{:S(2)}) copy-start(bf16[128,8,128]{2,1,0:T(8,128)(2,1)} %param.9) | copy-start | bytes 786436
  0.6 2.0 %copy-start.3 = (bf16[128,8,128]{2,1,0:T(8,128)(2,1)S(1)}, bf16[128,8,128]{2,1,0:T(8,128)(2,1)}, u32[]{:S(2)}) copy-start(bf16[128,8,128]{2,1,0:T(8,128)(2,1)} %param.8) | copy-start | bytes 786436
  63.8 0.7 copy-start.4
  65.7 1.9 %copy-start.1 = (f32[8,64,128]{2,1,0:T(8,128)S(1)}, f32[8,64,128]{2,1,0:T(8,128)}, u32[]{:S(2)}) copy-start(f32[8,64,128]{2,1,0:T(8,128)} %get-tuple-element.26) | copy-start | bytes 786436
  67.6 1.0 %copy-start = (f32[8,64,128]{2,1,0:T(8,128)S(1)}, f32[8,64,128]{2,1,0:T(8,128)}, u32[]{:S(2)}) copy-start(f32[8,64,128]{2,1,0:T(8,128)} %get-tuple-element.27) | copy-start | bytes 786436

commit v2 on v1

--- a/solution.py
+++ b/solution.py
@@ -63,10 +63,12 @@
 
 
 def kernel(
-    q_in, k_in, v_in, t_in, wq_ref, wk_ref,
-    stu_out, gq_out, gk_out, loss_out,
-    kbuf, vbuf, qbuf, tbuf, fkt, fkb, fqt, fqb, vta, pre, tot, win, lin, gna, gfk, later,
-    own1, ag1, own2, ag2, stu, rs_own, rs_got, fin, la, lb, lc, scal,
+    q_hbm, k_hbm, v_hbm, t_hbm, wq_hbm, wk_hbm,
+    stu_out, fin_out, loss_out,
+    xin, xs, wq_ref, wk_ref,
+    kbuf, vbuf, qbuf, tbuf, fkt, fkb, fqt, fqb, vta, pre, tot, win, outs, lin, gna, gfk, later,
+    own1, ag1, own2, ag2, stu, stu_got, stu_t, rs_own, rs_got, fin, la, lb, lc, scal,
+    in_sem, w_sem, out_sem,
     x_send, x_recv, h_send, h_recv, a1_send, a1_recv, a2_send, a2_recv,
     s_send, s_recv, r_send, r_recv, f_send, f_recv, l_send, l_recv,
 ):
@@ -80,16 +82,47 @@
     def ctx(i):
         return {"ctx": i}
 
+    y, z, c = me // 16, h, lax.rem(me, 2)
+    k_in, v_in, q_in, t_in = (xs.at[a] for a in range(4))
+    loads = [pltpu.make_async_copy(src, xin.at[a], in_sem.at[a]) for a, src in enumerate((k_hbm, v_hbm, q_hbm, t_hbm))]
+    weights = [
+        pltpu.make_async_copy(wq_hbm, wq_ref, w_sem.at[0]),
+        pltpu.make_async_copy(wk_hbm, wk_ref, w_sem.at[1]),
+    ]
+    for load in loads + weights:
+        load.start()
+
     bar = pltpu.get_barrier_semaphore()
 
-    def greet(o, _):
-        pl.semaphore_signal(bar, inc=1, device_id=ctx(lax.rem(me + o, 64)), device_id_type=MESH)
-        return 0
-
-    lax.fori_loop(1, 64, greet, 0)
+    def greet(device):
+        pl.semaphore_signal(bar, inc=1, device_id=device, device_id_type=MESH)
+
+    for o in FAR:
+        for d in range(2):
+            if o or d:
+                greet(ctx(16 * y + 2 * lax.rem(z + o, NB) + lax.rem(c + d, 2)))
     for o in range(1, 4):
-        pl.semaphore_signal(bar, inc=1, device_id={"head": lax.rem(xme + o, 4)}, device_id_type=MESH)
-    pl.semaphore_wait(bar, 66)
+        for d in range(2):
+            greet(ctx(16 * lax.rem(y + o, 4) + 2 * z + d))
+        greet({"head": lax.rem(xme + o, 4)})
+    gives = jnp.logical_and(lax.rem(me, 16) == 15, y < 3)
+    takes = jnp.logical_and(c == 0, y > 0)
+
+    @pl.when(gives)
+    def _():
+        for o in range(NB):
+            greet(ctx(16 * (y + 1) + 2 * o))
+
+    @pl.when(takes)
+    def _():
+        greet(ctx(16 * (y - 1) + 15))
+
+    for a in range(4):
+        loads[a].wait()
+        xs[a] = jnp.swapaxes(xin[a], 0, 1)
+    for load in weights:
+        load.wait()
+    pl.semaphore_wait(bar, 24 + 8 * gives.astype(jnp.int32) + takes.astype(jnp.int32))
 
     arrays = ((k_in, kbuf, WIN), (v_in, vbuf, WIN), (q_in, qbuf, 0), (t_in, tbuf, 0))
 
@@ -268,55 +301,41 @@
             lin[...] += ag1[m].astype(F32)
     carry = joined(lin[...])
     carry_b = split(carry)
-    arrived(3)
-
-    la[b] = jnp.zeros((8, CH), F32)
-    later[NB - 1] = jnp.zeros((AUG, CH), F32)
-
-    def out_chunk(k):
-        n = NB - 1 - k
-        ls = scal[n][:1]
-        full = win[n] + ls * nn(carry_b, fqb[n])
+
+    def out_chunk(n):
+        full = win[n] + scal[n][:1] * nn(carry_b, fqb[n])
         inv = 1.0 / full[HD : HD + 1]
         out = full[:HD] * inv
+        outs[n] = out
         stu[n] = nt(eye, out.astype(BF)).astype(BF)
+        scal[n] = jnp.broadcast_to(scal[n][:1] * inv, (8, CH))
+
+    each(out_chunk)
+    arrived(3)
+    errors, suffix = [], [jnp.zeros((AUG, CH), F32)]
+
+    def diff_chunk(k):
+        n = NB - 1 - k
+        coef, out = scal[n][:1], outs[n]
         diff = out - nt(eye, tbuf[pl.ds(n * CH, CH)])
         sq = diff * diff
-        acc = sq[0:8]
-        for r in range(1, HD // 8):
-            acc = acc + sq[8 * r : 8 * r + 8]
-        la[b] += acc
-        coef = ls * inv
+        for r in range(HD // 8):
+            errors.append(sq[8 * r : 8 * r + 8])
         g = diff * (2.0 / HD)
         gd = -coef * jnp.sum(g * out, axis=0, keepdims=True)
         scal[n] = jnp.broadcast_to(gd, (8, CH))
         ga = jnp.concatenate([coef * g, gd * one_row], axis=0).astype(BF)
         gna[n] = ga
-        step = nt(ga, fqb[n])
-        if n > 0:
-            later[n - 1] = later[n] + step
-        else:
-            own2[...] = split(later[0] + step)
-
-    each(out_chunk)
+        later[n] = suffix[-1]
+        suffix.append(suffix[-1] + nt(ga, fqb[n]))
+
+    each(diff_chunk)
+    own2[...] = split(suffix[-1])
+    while len(errors) > 1:
+        errors = [sum(errors[i : i + 2]) for i in range(0, len(errors), 2)]
+    la[b] = errors[0]
     for o in range(7, 0, -1):
         backward(o, go)
-
-    def student(j, act):
-        to = NB * b + j
-
-        def remote():
-            act(pltpu.make_async_remote_copy(
-                stu.at[j], stu_out.at[h], s_send.at[j], s_recv, device_id=ctx(to), device_id_type=MESH))
-
-        pl.when(to != me)(remote)
-        if act is go:
-            @pl.when(to == me)
-            def _():
-                pltpu.make_async_copy(stu.at[j], stu_out.at[h], s_recv).start()
-
-    for j in range(NB):
-        student(j, go)
 
     def loss_a(o, act):
         act(pltpu.make_async_remote_copy(
@@ -343,6 +362,22 @@
 
     for o in range(1, NB):
         loss_a(o, go)
+
+    def student(j, act):
+        to = NB * b + j
+
+        def remote():
+            act(pltpu.make_async_remote_copy(
+                stu.at[j], stu_got.at[h], s_send.at[j], s_recv, device_id=ctx(to), device_id_type=MESH))
+
+        pl.when(to != me)(remote)
+        if act is go:
+            @pl.when(to == me)
+            def _():
+                pltpu.make_async_copy(stu.at[j], stu_got.at[h], s_recv).start()
+
+    for j in range(NB):
+        student(j, go)
 
     dq = []
 
@@ -361,9 +396,17 @@
     grad_q = nn(jnp.concatenate(dq, axis=1), qbuf[...])
     rs_own[pl.ds(0, HF)] = grad_q.astype(BF)
 
-    lb[xme] = total(la, NB, 0)
-    for o in range(1, 4):
-        loss_b(o, go)
+    def reduce(o, act, keys):
+        m = lax.rem(b + o, NB)
+
+        @pl.when((m >= 4) if keys else (m < 4))
+        def _():
+            act(pltpu.make_async_remote_copy(
+                rs_own.at[pl.ds(pl.multiple_of(16 * m, 16), 16)], rs_got.at[b], r_send.at[o], r_recv,
+                device_id=ctx(place(m, h)), device_id_type=MESH))
+
+    for o in range(1, NB):
+        reduce(o, go, False)
 
     lin[...] = jnp.zeros((AUG, CH), F32)
     for m in range(1, NB):
@@ -381,35 +424,37 @@
     grad_k = nn(jnp.concatenate(dk, axis=1), kbuf[pl.ds(0, NB * CH)])
     rs_own[pl.ds(HF, HF)] = grad_k.astype(BF)
 
-    def reduce(o, act):
-        m = lax.rem(b + o, NB)
-        act(pltpu.make_async_remote_copy(
-            rs_own.at[pl.ds(pl.multiple_of(16 * m, 16), 16)], rs_got.at[b], r_send.at[o], r_recv,
-            device_id=ctx(place(m, h)), device_id_type=MESH))
-
     for o in range(1, NB):
-        reduce(o, go)
+        reduce(o, go, True)
     rs_got[b] = rs_own[pl.ds(pl.multiple_of(16 * b, 16), 16)]
-    lc[h] = total(lb, 4, 1)
-    for o in range(1, NB):
-        loss_c(o, go)
+    lb[xme] = total(la, NB, 0)
+    for o in range(1, 4):
+        loss_b(o, go)
     part = rs_got.at[pl.ds(0, NB - 1)]
     pltpu.make_async_copy(part, part, r_recv).wait()
     acc = rs_got[0].astype(F32)
     for m in range(1, NB):
         acc = acc + rs_got[m].astype(F32)
+    fin[...] = acc.astype(BF)
     slot = NB * h + b
-    fin[slot] = acc.astype(BF)
-
-    def spread(o, _):
-        pltpu.make_async_remote_copy(
-            fin.at[slot], fin.at[slot], f_send, f_recv,
-            device_id=ctx(lax.rem(me + o, 64)), device_id_type=MESH).start()
-        return 0
-
-    lax.fori_loop(1, 64, spread, 0)
-
-    loss_out[...] = total(lc, NB, 2)
+
+    for o in FAR:
+        for p in (2, 1, 3, 0):
+            for d in range(2):
+                if o or p or d:
+                    pltpu.make_async_remote_copy(
+                        fin, fin_out.at[slot], f_send, f_recv,
+                        device_id=ctx(16 * lax.rem(y + p, 4) + 2 * lax.rem(z + o, NB) + lax.rem(c + d, 2)),
+                        device_id_type=MESH).start()
+    pltpu.make_async_copy(fin, fin_out.at[slot], f_recv).start()
+
+    lc[h] = total(lb, 4, 1)
+    for o in range(1, NB):
+        loss_c(o, go)
+    pltpu.make_async_copy(stu_got, stu_got, s_recv).wait()
+    stu_t[...] = jnp.swapaxes(stu_got[...], 0, 1)
+    put = pltpu.make_async_copy(stu_t, stu_out, out_sem)
+    put.start()
 
     for o in range(NB):
         for a in range(4):
@@ -426,37 +471,36 @@
         backward(o, sent)
         loss_a(o, sent)
         loss_c(o, sent)
-        reduce(o, sent)
+        reduce(o, sent, False)
+        reduce(o, sent, True)
     for o in range(1, 4):
         loss_b(o, sent)
     for j in range(NB):
         student(j, sent)
-    pltpu.make_async_copy(stu_out, stu_out, s_recv).wait()
-    part = fin.at[pl.ds(0, 63)]
+    loss_out[0, 0] = jnp.sum(total(lc, NB, 2)) * (1.0 / (8192 * 32 * 128))
+    put.wait()
+    part = fin_out.at[pl.ds(0, 63)]
     pltpu.make_async_copy(part, part, f_send).wait()
-    pltpu.make_async_copy(part, part, f_recv).wait()
-    for d in range(NB):
-        for m in range(4):
-            gq_out[d, pl.ds(16 * m, 16)] = fin[NB * d + m].astype(F32)
-            gk_out[d, pl.ds(16 * m, 16)] = fin[NB * d + 4 + m].astype(F32)
+    pltpu.make_async_copy(fin_out, fin_out, f_recv).wait()
 
 
 def per_device(queries, keys, values, teacher, wq, wk):
-    heads = [jnp.swapaxes(x, 0, 1) for x in (queries, keys, values, teacher)]
-    vm = pl.BlockSpec(memory_space=pltpu.VMEM)
     hbm = pl.BlockSpec(memory_space=pl.ANY)
     dma = pltpu.SemaphoreType.DMA
-    stu, gq, gk, loss = pl.pallas_call(
+    stu, fin, loss = pl.pallas_call(
         kernel,
         out_shape=(
-            jax.ShapeDtypeStruct((NB, CH, HD), BF),
-            jax.ShapeDtypeStruct((NB, HF, HD), F32),
-            jax.ShapeDtypeStruct((NB, HF, HD), F32),
-            jax.ShapeDtypeStruct((8, CH), F32),
+            jax.ShapeDtypeStruct((CH, NB, HD), BF),
+            jax.ShapeDtypeStruct((NB * NB, 16, HD), BF),
+            jax.ShapeDtypeStruct((1, 1), F32),
         ),
-        in_specs=[hbm] * 4 + [vm] * 2,
-        out_specs=(vm, vm, vm, vm),
+        in_specs=[hbm] * 6,
+        out_specs=(hbm, hbm, pl.BlockSpec(memory_space=pltpu.SMEM)),
         scratch_shapes=[
+            pltpu.VMEM((4, CH, NB, HD), BF),
+            pltpu.VMEM((4, NB, CH, HD), BF),
+            pltpu.VMEM((NB, HF, HD), BF),
+            pltpu.VMEM((NB, HF, HD), BF),
             pltpu.VMEM((NB * CH + WIN, HD), BF),
             pltpu.VMEM((NB * CH + WIN, HD), BF),
             pltpu.VMEM((NB * CH, HD), BF),
@@ -469,6 +513,7 @@
             pltpu.VMEM((NB, AUG, CH), F32),
             pltpu.VMEM((AUG, CH), F32),
             pltpu.VMEM((NB, AUG, CH), F32),
+            pltpu.VMEM((NB, HD, CH), F32),
             pltpu.VMEM((AUG, CH), F32),
             pltpu.VMEM((NB, AUG, CH), BF),
             pltpu.VMEM((NB, CH, CH), F32),
@@ -478,13 +523,16 @@
             pltpu.VMEM((AUG, CH), BF),
             pltpu.VMEM((NB, AUG, CH), BF),
             pltpu.VMEM((NB, CH, HD), BF),
+            pltpu.VMEM((NB, CH, HD), BF),
+            pltpu.VMEM((CH, NB, HD), BF),
             pltpu.VMEM((2 * HF, HD), BF),
             pltpu.VMEM((NB, 16, HD), BF),
-            pltpu.VMEM((NB * NB, 16, HD), BF),
+            pltpu.VMEM((16, HD), BF),
             pltpu.VMEM((NB, 8, CH), F32),
             pltpu.VMEM((4, 8, CH), F32),
             pltpu.VMEM((NB, 8, CH), F32),
             pltpu.VMEM((NB, 8, CH), F32),
+            dma((4,)), dma((2,)), dma,
             dma((4, NB)), dma((4,)),
             dma((2, NB)), dma((2,)),
             dma((NB,)), dma((NB,)),
@@ -495,9 +543,9 @@
             dma((3, NB)), dma((3,)),
         ],
         compiler_params=pltpu.CompilerParams(collective_id=0, has_side_effects=True),
-    )(*heads, wq, wk)
-    entries = 8192 * 32 * 128
-    return jnp.swapaxes(stu, 0, 1), jnp.sum(loss) / entries, gq, gk
+    )(queries, keys, values, teacher, wq, wk)
+    grads = fin.reshape(NB, 2 * HF, HD)
+    return stu, loss[0, 0], grads[:, :HF].astype(F32), grads[:, HF:].astype(F32)
 
 
 def solution(mesh):

time: 70.7 us -> 62 us (0.88)
  local copies, waits for them, and re-layouts: 7.15 us -> 0.71 us
  Pallas kernels: 60.3 us -> 56.9 us
  other arithmetic: 0.6 us -> 1.85 us
    unnamed x13 -> x3, local copies, waits for them, and re-layouts: 4.29 us -> 0.71 us
    pallas_call x1, Pallas kernels: 60.3 us -> 56.9 us  [per_device(): pl.pallas_call(kernel, out_shape=(jax.ShapeDtypeStruct((CH, NB, HD), BF),...]
    transpose x2 -> x0, local copies, waits for them, and re-layouts: 2.85 us -> none  [per_device(): heads = [jnp.swapaxes(x, 0, 1) for x in (queries, keys, values, teacher)]]
    convert_element_type x0 -> x1, other arithmetic: none -> 1.85 us  [per_device(): grads[:, HF:].astype(F32)]
where the time goes in v2:
time: 62 us; the launch traced here: 61.9 us
  Pallas kernels  56.9 us (92%)
  between operations  2.39 us (4%)
  other arithmetic  1.85 us (3%)
  local copies, waits for them, and re-layouts  0.71 us (1%)
    pallas_call x1, Pallas kernels, per_device(): pl.pallas_call(kernel, out_shape=(jax.ShapeDtypeStruct((CH, NB, HD), BF),...  56.9 us
    convert_element_type x1, other arithmetic, per_device(): grads[:, HF:].astype(F32)  1.85 us

profile of v2, /device:TPU:1, one launch (start us, length us, event | category | flops | bytes accessed | tf_op | source)
XLA Modules:
  0.0 61.9 jit_solution(11687157996324208780)
XLA Ops:
  0.6 56.9 %shard_map.93 = (bf16[128,8,128]{2,1,0:T(8,128)(2,1)}, bf16[64,16,128]{2,1,0:T(8,128)(2,1)}, f32[1,1]{1,0:T(1,128)}) custom-call(bf16[128,8,128]{2,1,0:T(8,128)(2,1)} %q_hbm.1, bf16[128,8,128]{2,1,0:T(8,128)(2,1)} %k_hbm.1, bf16[128,8,128]{2,1,0:T(8,128)(2,1)} %v_hbm.1, bf16[128,8,128]{2,1,0:T(8,128)(2,1)} %t_hbm.1, bf16[8,64,128]{2,1,0:T(8,128)(2,1)} %wq_hbm.1, ...), custom_call_target="tpu_custom_call" | custom-call | tf_op jit(solution)/shard_map/pallas_call | solution.py:490
  57.6 0.0 copy-start
  57.6 1.9 %slice_convert_fusion = (f32[8,64,128]{2,1,0:T(8,128)}, f32[8,64,128]{2,1,0:T(8,128)}) fusion(bf16[8,128,128]{2,1,0:T(8,128)(2,1)} %bitcast.2), kind=kLoop, calls=%fused_computation | loop fusion | flops 131072 | bytes 786432 | tf_op jit(solution)/shard_map/convert_element_type | solution.py:548
  59.4 0.0 copy-done
  59.4 0.7 %copy.12 = bf16[128,8,128]{2,1,0:T(8,128)(2,1)} copy(bf16[128,8,128]{2,1,0:T(8,128)(2,1)S(1)} %copy-done) | data formatting | bytes 524288
Async XLA Ops:
  57.6 1.9 %copy-start = (bf16[128,8,128]{2,1,0:T(8,128)(2,1)S(1)}, bf16[128,8,128]{2,1,0:T(8,128)(2,1)}, u32[]{:S(2)}) copy-start(bf16[128,8,128]{2,1,0:T(8,128)(2,1)} %get-tuple-element.16) | copy-start | bytes 786436

commit v3 on v2

--- a/solution.py
+++ b/solution.py
@@ -66,9 +66,9 @@
     q_hbm, k_hbm, v_hbm, t_hbm, wq_hbm, wk_hbm,
     stu_out, fin_out, loss_out,
     xin, xs, wq_ref, wk_ref,
-    kbuf, vbuf, qbuf, tbuf, fkt, fkb, fqt, fqb, vta, pre, tot, win, outs, lin, gna, gfk, later,
-    own1, ag1, own2, ag2, stu, stu_got, stu_t, rs_own, rs_got, fin, la, lb, lc, scal,
-    in_sem, w_sem, out_sem,
+    kbuf, vbuf, qbuf, tbuf, fkt, fkb, fqt, fqb, vta, pre, win, outs, lin, gna, gfk, later,
+    own1, ag1, own2, ag2, stu, stu_got, stu_t, gsum, fin, la, lb, lc, loss, scal,
+    in_sem, w_sem, out_sem, loss_sem,
     x_send, x_recv, h_send, h_recv, a1_send, a1_recv, a2_send, a2_recv,
     s_send, s_recv, r_send, r_recv, f_send, f_recv, l_send, l_recv,
 ):
@@ -89,8 +89,6 @@
         pltpu.make_async_copy(wq_hbm, wq_ref, w_sem.at[0]),
         pltpu.make_async_copy(wk_hbm, wk_ref, w_sem.at[1]),
     ]
-    for load in loads + weights:
-        load.start()
 
     bar = pltpu.get_barrier_semaphore()
 
@@ -117,6 +115,8 @@
     def _():
         greet(ctx(16 * (y - 1) + 15))
 
+    for load in loads + weights:
+        load.start()
     for a in range(4):
         loads[a].wait()
         xs[a] = jnp.swapaxes(xin[a], 0, 1)
@@ -134,7 +134,7 @@
 
         def remote():
             act(pltpu.make_async_remote_copy(
-                src.at[hd], rows, x_send.at[a, o], x_recv.at[a], device_id=ctx(to), device_id_type=MESH))
+                src.at[hd], rows, x_send.at[a], x_recv.at[a], device_id=ctx(to), device_id_type=MESH))
 
         if o == 0:
             pl.when(to != me)(remote)
@@ -160,7 +160,7 @@
 
         def remote():
             act(pltpu.make_async_remote_copy(
-                src.at[hd, pl.ds(CH - WIN, WIN)], dst.at[pl.ds(0, WIN)], h_send.at[a, o], h_recv.at[a],
+                src.at[hd, pl.ds(CH - WIN, WIN)], dst.at[pl.ds(0, WIN)], h_send.at[a], h_recv.at[a],
                 device_id=ctx(to), device_id_type=MESH))
 
         if o == 0:
@@ -173,19 +173,14 @@
         else:
             remote()
 
-    for o in FAR:
-        exchange(0, o, go)
-        exchange(1, o, go)
-
-    @pl.when(tail)
-    def _():
-        for o in FAR:
-            halo(0, o, go)
-            halo(1, o, go)
-
-    for a in (2, 3):
+    for a in range(4):
         for o in FAR:
             exchange(a, o, go)
+        if a < 2:
+            @pl.when(tail)
+            def _():
+                for o in FAR:
+                    halo(a, o, go)
 
     @pl.when(first_block)
     def _():
@@ -211,18 +206,16 @@
         pltpu.make_async_copy(part, part, h_recv.at[a]).wait()
 
     arrived(0)
-    arrived(1)
 
     @pl.when(b > 0)
     def _():
         halo_arrived(0)
-        halo_arrived(1)
 
     cidx = lax.broadcasted_iota(jnp.int32, (CH, CH), 0)
     iidx = lax.broadcasted_iota(jnp.int32, (CH, CH), 1)
     lower = cidx <= iidx
 
-    tot[...] = jnp.zeros((AUG, CH), F32)
+    sums = [jnp.zeros((AUG, CH), F32)]
 
     def key_chunk(n):
         f = halves(nt(w2k, kbuf[pl.ds(n * CH, CH)]))
@@ -233,15 +226,24 @@
         fb = f.astype(BF)
         fk = nt(eye, fb).astype(BF)
         fkb[n] = fk
+
+    each(key_chunk)
+    arrived(1)
+
+    @pl.when(b > 0)
+    def _():
+        halo_arrived(1)
+
+    def value_chunk(n):
         va = jnp.concatenate([nt(eye, vbuf[pl.ds(n * CH, CH)]), one_row], axis=0).astype(BF)
         vta[n] = va
-        pre[n] = tot[...]
-        tot[...] += nn(va, fk)
-
-    each(key_chunk)
+        pre[n] = sums[-1]
+        sums.append(sums[-1] + nn(va, fkb[n]))
+
+    each(value_chunk)
     vta[NB, :, pl.ds(0, WIN)] = jnp.concatenate(
         [nt(eye, vbuf[pl.ds(NB * CH, WIN)]), one_row[:, :WIN]], axis=0).astype(BF)
-    own1[...] = split(tot[...])
+    own1[...] = split(sums[-1])
 
     def scan_copy(o, own, got, send, recv):
         return pltpu.make_async_remote_copy(
@@ -307,7 +309,6 @@
         inv = 1.0 / full[HD : HD + 1]
         out = full[:HD] * inv
         outs[n] = out
-        stu[n] = nt(eye, out.astype(BF)).astype(BF)
         scal[n] = jnp.broadcast_to(scal[n][:1] * inv, (8, CH))
 
     each(out_chunk)
@@ -339,17 +340,17 @@
 
     def loss_a(o, act):
         act(pltpu.make_async_remote_copy(
-            la.at[b], la.at[b], l_send.at[0, o], l_recv.at[0],
+            la.at[b], la.at[b], l_send.at[0], l_recv.at[0],
             device_id=ctx(place(lax.rem(b + o, NB), h)), device_id_type=MESH))
 
     def loss_b(o, act):
         act(pltpu.make_async_remote_copy(
-            lb.at[xme], lb.at[xme], l_send.at[1, o], l_recv.at[1],
+            lb.at[xme], lb.at[xme], l_send.at[1], l_recv.at[1],
             device_id={"head": lax.rem(xme + o, 4)}, device_id_type=MESH))
 
     def loss_c(o, act):
         act(pltpu.make_async_remote_copy(
-            lc.at[h], lc.at[h], l_send.at[2, o], l_recv.at[2],
+            lc.at[h], lc.at[h], l_send.at[2], l_recv.at[2],
             device_id=ctx(place(b, lax.rem(h + o, NB))), device_id_type=MESH))
 
     def total(ref, count, level):
@@ -368,7 +369,7 @@
 
         def remote():
             act(pltpu.make_async_remote_copy(
-                stu.at[j], stu_got.at[h], s_send.at[j], s_recv, device_id=ctx(to), device_id_type=MESH))
+                stu.at[j], stu_got.at[h], s_send, s_recv, device_id=ctx(to), device_id_type=MESH))
 
         pl.when(to != me)(remote)
         if act is go:
@@ -376,6 +377,8 @@
             def _():
                 pltpu.make_async_copy(stu.at[j], stu_got.at[h], s_recv).start()
 
+    for j in range(NB):
+        stu[j] = nt(eye, outs[j].astype(BF)).astype(BF)
     for j in range(NB):
         student(j, go)
 
@@ -393,20 +396,36 @@
         gfk[n] = nt(fqb[n], mx) + nn(lt, vta[n])
 
     each(mix_chunk)
-    grad_q = nn(jnp.concatenate(dq, axis=1), qbuf[...])
-    rs_own[pl.ds(0, HF)] = grad_q.astype(BF)
-
-    def reduce(o, act, keys):
-        m = lax.rem(b + o, NB)
-
-        @pl.when((m >= 4) if keys else (m < 4))
-        def _():
-            act(pltpu.make_async_remote_copy(
-                rs_own.at[pl.ds(pl.multiple_of(16 * m, 16), 16)], rs_got.at[b], r_send.at[o], r_recv,
-                device_id=ctx(place(m, h)), device_id_type=MESH))
+    gsum[0, b] = nn(jnp.concatenate(dq, axis=1), qbuf[...]).astype(BF)
+
+    def share(w, o, act):
+        act(pltpu.make_async_remote_copy(
+            gsum.at[w, b], gsum.at[w, b], r_send.at[w], r_recv.at[w],
+            device_id=ctx(place(lax.rem(b + o, NB), h)), device_id_type=MESH))
+
+    def summed(w):
+        part = gsum.at[w, pl.ds(0, NB - 1)]
+        pltpu.make_async_copy(part, part, r_recv.at[w]).wait()
+        acc = gsum[w, 0].astype(F32)
+        for m in range(1, NB):
+            acc = acc + gsum[w, m].astype(F32)
+        fin[w] = acc.astype(BF)
+
+    def spread(w, o, act):
+        act(pltpu.make_async_remote_copy(
+            fin.at[w], fin_out.at[w, h], f_send.at[w], f_recv.at[w],
+            device_id=ctx(place(b, lax.rem(h + o, NB))), device_id_type=MESH))
+
+    def spread_all(w):
+        for o in FAR[:-1]:
+            spread(w, o, go)
+        pltpu.make_async_copy(fin.at[w], fin_out.at[w, h], f_recv.at[w]).start()
 
     for o in range(1, NB):
-        reduce(o, go, False)
+        share(0, o, go)
+    lb[xme] = total(la, NB, 0)
+    for o in range(1, 4):
+        loss_b(o, go)
 
     lin[...] = jnp.zeros((AUG, CH), F32)
     for m in range(1, NB):
@@ -421,32 +440,13 @@
         dk.append(proj_grad(fkt[n], gfk[n] + nn(after, vta[n])))
 
     each(key_grad)
-    grad_k = nn(jnp.concatenate(dk, axis=1), kbuf[pl.ds(0, NB * CH)])
-    rs_own[pl.ds(HF, HF)] = grad_k.astype(BF)
-
+    gsum[1, b] = nn(jnp.concatenate(dk, axis=1), kbuf[pl.ds(0, NB * CH)]).astype(BF)
     for o in range(1, NB):
-        reduce(o, go, True)
-    rs_got[b] = rs_own[pl.ds(pl.multiple_of(16 * b, 16), 16)]
-    lb[xme] = total(la, NB, 0)
-    for o in range(1, 4):
-        loss_b(o, go)
-    part = rs_got.at[pl.ds(0, NB - 1)]
-    pltpu.make_async_copy(part, part, r_recv).wait()
-    acc = rs_got[0].astype(F32)
-    for m in range(1, NB):
-        acc = acc + rs_got[m].astype(F32)
-    fin[...] = acc.astype(BF)
-    slot = NB * h + b
-
-    for o in FAR:
-        for p in (2, 1, 3, 0):
-            for d in range(2):
-                if o or p or d:
-                    pltpu.make_async_remote_copy(
-                        fin, fin_out.at[slot], f_send, f_recv,
-                        device_id=ctx(16 * lax.rem(y + p, 4) + 2 * lax.rem(z + o, NB) + lax.rem(c + d, 2)),
-                        device_id_type=MESH).start()
-    pltpu.make_async_copy(fin, fin_out.at[slot], f_recv).start()
+        share(1, o, go)
+    summed(0)
+    spread_all(0)
+    summed(1)
+    spread_all(1)
 
     lc[h] = total(lb, 4, 1)
     for o in range(1, NB):
@@ -456,46 +456,75 @@
     put = pltpu.make_async_copy(stu_t, stu_out, out_sem)
     put.start()
 
-    for o in range(NB):
-        for a in range(4):
-            exchange(a, o, sent)
-
-    @pl.when(tail)
-    def _():
-        for o in range(NB):
-            halo(0, o, sent)
-            halo(1, o, sent)
+    def left(ref, sem):
+        pltpu.make_async_copy(ref, ref, sem).wait()
+
+    own = (me == place(src_b, h)).astype(jnp.int32)
+    for n in range(2):
+        @pl.when(own == n)
+        def _():
+            for a in range(4):
+                left(qbuf.at[pl.ds(0, CH * (NB - n))], x_send.at[a])
+            left(stu.at[pl.ds(0, NB - n)], s_send)
+
+        @pl.when(jnp.logical_and(tail, (me == place(src_b + 1, h)).astype(jnp.int32) == n))
+        def _():
+            for a in range(2):
+                left(qbuf.at[pl.ds(0, WIN * (NB - n))], h_send.at[a])
 
     for o in range(1, NB):
         forward(o, sent)
         backward(o, sent)
-        loss_a(o, sent)
-        loss_c(o, sent)
-        reduce(o, sent, False)
-        reduce(o, sent, True)
-    for o in range(1, 4):
-        loss_b(o, sent)
-    for j in range(NB):
-        student(j, sent)
-    loss_out[0, 0] = jnp.sum(total(lc, NB, 2)) * (1.0 / (8192 * 32 * 128))
+    left(la.at[pl.ds(0, NB - 1)], l_send.at[0])
+    left(lb.at[pl.ds(0, 3)], l_send.at[1])
+    left(lc.at[pl.ds(0, NB - 1)], l_send.at[2])
+    for w in range(2):
+        left(gsum.at[w, pl.ds(0, NB - 1)], r_send.at[w])
+        left(gsum.at[w, pl.ds(0, NB - 1)], f_send.at[w])
+    loss[...] = jnp.sum(total(lc, NB, 2), keepdims=True) * (1.0 / (8192 * 32 * 128))
+    put_loss = pltpu.make_async_copy(loss, loss_out, loss_sem)
+    put_loss.start()
     put.wait()
-    part = fin_out.at[pl.ds(0, 63)]
-    pltpu.make_async_copy(part, part, f_send).wait()
-    pltpu.make_async_copy(fin_out, fin_out, f_recv).wait()
+    put_loss.wait()
+    for w in range(2):
+        pltpu.make_async_copy(fin_out.at[w], fin_out.at[w], f_recv.at[w]).wait()
+
+
+def finish(stu_in, fin_in, loss_in, stu_out, gq_out, gk_out, loss_out, fin, gq, gk, loss, in_sem, out_sem):
+    loads = [
+        pltpu.make_async_copy(src, dst, in_sem.at[i])
+        for i, (src, dst) in enumerate(((fin_in, fin), (loss_in, loss)))
+    ]
+    stores = [
+        pltpu.make_async_copy(src, dst, out_sem.at[i])
+        for i, (src, dst) in enumerate(((gq, gq_out), (gk, gk_out), (loss, loss_out), (stu_in, stu_out)))
+    ]
+    for load in loads:
+        load.start()
+    stores[3].start()
+    loads[0].wait()
+    gq[...] = fin[0].astype(F32)
+    stores[0].start()
+    gk[...] = fin[1].astype(F32)
+    stores[1].start()
+    loads[1].wait()
+    stores[2].start()
+    for store in stores:
+        store.wait()
 
 
 def per_device(queries, keys, values, teacher, wq, wk):
-    hbm = pl.BlockSpec(memory_space=pl.ANY)
+    anywhere = pl.BlockSpec(memory_space=pl.ANY)
     dma = pltpu.SemaphoreType.DMA
     stu, fin, loss = pl.pallas_call(
         kernel,
         out_shape=(
             jax.ShapeDtypeStruct((CH, NB, HD), BF),
-            jax.ShapeDtypeStruct((NB * NB, 16, HD), BF),
+            jax.ShapeDtypeStruct((2, NB, HF, HD), BF),
             jax.ShapeDtypeStruct((1, 1), F32),
         ),
-        in_specs=[hbm] * 6,
-        out_specs=(hbm, hbm, pl.BlockSpec(memory_space=pltpu.SMEM)),
+        in_specs=[anywhere] * 6,
+        out_specs=(anywhere,) * 3,
         scratch_shapes=[
             pltpu.VMEM((4, CH, NB, HD), BF),
             pltpu.VMEM((4, NB, CH, HD), BF),
@@ -511,7 +540,6 @@
             pltpu.VMEM((NB, CH, CH), BF),
             pltpu.VMEM((NB + 1, AUG, CH), BF),
             pltpu.VMEM((NB, AUG, CH), F32),
-            pltpu.VMEM((AUG, CH), F32),
             pltpu.VMEM((NB, AUG, CH), F32),
             pltpu.VMEM((NB, HD, CH), F32),
             pltpu.VMEM((AUG, CH), F32),
@@ -525,27 +553,47 @@
             pltpu.VMEM((NB, CH, HD), BF),
             pltpu.VMEM((NB, CH, HD), BF),
             pltpu.VMEM((CH, NB, HD), BF),
-            pltpu.VMEM((2 * HF, HD), BF),
-            pltpu.VMEM((NB, 16, HD), BF),
-            pltpu.VMEM((16, HD), BF),
+            pltpu.VMEM((2, NB, HF, HD), BF),
+            pltpu.VMEM((2, HF, HD), BF),
             pltpu.VMEM((NB, 8, CH), F32),
             pltpu.VMEM((4, 8, CH), F32),
             pltpu.VMEM((NB, 8, CH), F32),
+            pltpu.VMEM((1, 1), F32),
             pltpu.VMEM((NB, 8, CH), F32),
-            dma((4,)), dma((2,)), dma,
-            dma((4, NB)), dma((4,)),
-            dma((2, NB)), dma((2,)),
+            dma((4,)), dma((2,)), dma, dma,
+            dma((4,)), dma((4,)),
+            dma((2,)), dma((2,)),
             dma((NB,)), dma((NB,)),
             dma((NB,)), dma((NB,)),
-            dma((NB,)), dma,
-            dma((NB,)), dma,
             dma, dma,
-            dma((3, NB)), dma((3,)),
+            dma((2,)), dma((2,)),
+            dma((2,)), dma((2,)),
+            dma((3,)), dma((3,)),
         ],
-        compiler_params=pltpu.CompilerParams(collective_id=0, has_side_effects=True),
-    )(queries, keys, values, teacher, wq, wk)
-    grads = fin.reshape(NB, 2 * HF, HD)
-    return stu, loss[0, 0], grads[:, :HF].astype(F32), grads[:, HF:].astype(F32)
+        compiler_params=pltpu.CompilerParams(
+            collective_id=0, has_side_effects=True, vmem_limit_bytes=24 * 2**20),
+    )(*(pltpu.with_memory_space_constraint(x, pltpu.HBM) for x in (queries, keys, values, teacher, wq, wk)))
+    stu, gq, gk, loss = pl.pallas_call(
+        finish,
+        out_shape=(
+            jax.ShapeDtypeStruct((CH, NB, HD), BF),
+            jax.ShapeDtypeStruct((NB, HF, HD), F32),
+            jax.ShapeDtypeStruct((NB, HF, HD), F32),
+            jax.ShapeDtypeStruct((1, 1), F32),
+        ),
+        in_specs=[anywhere] * 3,
+        out_specs=(anywhere,) * 4,
+        scratch_shapes=[
+            pltpu.VMEM((2, NB, HF, HD), BF),
+            pltpu.VMEM((NB, HF, HD), F32),
+            pltpu.VMEM((NB, HF, HD), F32),
+            pltpu.VMEM((1, 1), F32),
+            dma((2,)),
+            dma((4,)),
+        ],
+        compiler_params=pltpu.CompilerParams(vmem_limit_bytes=8 * 2**20),
+    )(stu, fin, loss)
+    return stu, loss[0, 0], gq, gk
 
 
 def solution(mesh):

time: 62 us -> 57.1 us (0.921)
  other arithmetic: 1.85 us -> 0 us
  between operations: 2.39 us -> 0.64 us
  local copies, waits for them, and re-layouts: 0.71 us -> 0 us
    pallas_call x1, Pallas kernels: 56.9 us -> 54.8 us  [per_device(): pl.pallas_call(kernel, out_shape=(jax.ShapeDtypeStruct((CH, NB, HD), BF),...]
    convert_element_type x1 -> x0, other arithmetic: 1.85 us -> none  [per_device(): grads[:, HF:].astype(F32)]
    pallas_call x0 -> x1, Pallas kernels: none -> 1.58 us  [per_device(): pl.pallas_call(finish, out_shape=(jax.ShapeDtypeStruct((CH, NB, HD), BF),...]
    unnamed x3 -> x0, local copies, waits for them, and re-layouts: 0.71 us -> none
where the time goes in v3:
time: 57.1 us; the launch traced here: 57 us
  Pallas kernels  56.3 us (99%)
  between operations  0.64 us (1%)
    pallas_call x1, Pallas kernels, per_device(): pl.pallas_call(kernel, out_shape=(jax.ShapeDtypeStruct((CH, NB, HD), BF),...  54.8 us
    pallas_call x1, Pallas kernels, per_device(): pl.pallas_call(finish, out_shape=(jax.ShapeDtypeStruct((CH, NB, HD), BF),...  1.58 us

profile of v3, /device:TPU:1, one launch (start us, length us, event | category | flops | bytes accessed | tf_op | source)
XLA Modules:
  0.0 57.0 jit_solution(10086265473470178152)
XLA Ops:
  0.6 54.8 %shard_map.93 = (bf16[128,8,128]{2,1,0:T(8,128)(2,1)S(1)}, bf16[2,8,64,128]{3,2,1,0:T(8,128)(2,1)S(1)}, f32[1,1]{1,0:T(1,128)}) custom-call(bf16[128,8,128]{2,1,0:T(8,128)(2,1)} %q_hbm.1, bf16[128,8,128]{2,1,0:T(8,128)(2,1)} %k_hbm.1, bf16[128,8,128]{2,1,0:T(8,128)(2,1)} %v_hbm.1, bf16[128,8,128]{2,1,0:T(8,128)(2,1)} %t_hbm.1, bf16[8,64,128]{2,1,0:T(8,128)(2,1)} %wq_hbm.1, ...), custom_call_target="tpu_custom_call" | custom-call | tf_op jit(solution)/shard_map/pallas_call | solution.py:519
  55.4 1.6 %shard_map.94 = (bf16[128,8,128]{2,1,0:T(8,128)(2,1)}, f32[8,64,128]{2,1,0:T(8,128)}, f32[8,64,128]{2,1,0:T(8,128)}, f32[1,1]{1,0:T(1,128)}) custom-call(bf16[128,8,128]{2,1,0:T(8,128)(2,1)S(1)} %get-tuple-element.11.stu_in, bf16[2,8,64,128]{3,2,1,0:T(8,128)(2,1)S(1)} %get-tuple-element.12.fin_in, f32[1,1]{1,0:T(1,128)} %get-tuple-element.13.loss_in), custom_call_target="tpu_custom_call" | custom-call | tf_op jit(solution)/shard_map/pallas_call | solution.py:576

commit v4 on v3

--- a/solution.py
+++ b/solution.py
@@ -67,10 +67,10 @@
     stu_out, fin_out, loss_out,
     xin, xs, wq_ref, wk_ref,
     kbuf, vbuf, qbuf, tbuf, fkt, fkb, fqt, fqb, vta, pre, win, outs, lin, gna, gfk, later,
-    own1, ag1, own2, ag2, stu, stu_got, stu_t, gsum, fin, la, lb, lc, loss, scal,
+    own1, ag1, own2, ag2, stu, stu_got, stu_t, gpart, gsum, fin, la, lb, lc, loss, scal, mask,
     in_sem, w_sem, out_sem, loss_sem,
-    x_send, x_recv, h_send, h_recv, a1_send, a1_recv, a2_send, a2_recv,
-    s_send, s_recv, r_send, r_recv, f_send, f_recv, l_send, l_recv,
+    x_send, x_recv, h_send, h_recv, a_send, a1_recv, a2_recv,
+    s_send, s_recv, r_send, r_recv, f_send, f_recv, g_send, g_recv, l_send, l_recv,
 ):
     me = lax.axis_index("ctx")
     xme = lax.axis_index("head")
@@ -103,18 +103,6 @@
         for d in range(2):
             greet(ctx(16 * lax.rem(y + o, 4) + 2 * z + d))
         greet({"head": lax.rem(xme + o, 4)})
-    gives = jnp.logical_and(lax.rem(me, 16) == 15, y < 3)
-    takes = jnp.logical_and(c == 0, y > 0)
-
-    @pl.when(gives)
-    def _():
-        for o in range(NB):
-            greet(ctx(16 * (y + 1) + 2 * o))
-
-    @pl.when(takes)
-    def _():
-        greet(ctx(16 * (y - 1) + 15))
-
     for load in loads + weights:
         load.start()
     for a in range(4):
@@ -122,7 +110,7 @@
         xs[a] = jnp.swapaxes(xin[a], 0, 1)
     for load in weights:
         load.wait()
-    pl.semaphore_wait(bar, 24 + 8 * gives.astype(jnp.int32) + takes.astype(jnp.int32))
+    pl.semaphore_wait(bar, 24)
 
     arrays = ((k_in, kbuf, WIN), (v_in, vbuf, WIN), (q_in, qbuf, 0), (t_in, tbuf, 0))
 
@@ -134,7 +122,7 @@
 
         def remote():
             act(pltpu.make_async_remote_copy(
-                src.at[hd], rows, x_send.at[a], x_recv.at[a], device_id=ctx(to), device_id_type=MESH))
+                src.at[hd], rows, x_send, x_recv.at[a], device_id=ctx(to), device_id_type=MESH))
 
         if o == 0:
             pl.when(to != me)(remote)
@@ -145,48 +133,38 @@
         else:
             remote()
 
+    def left(ref, sem):
+        pltpu.make_async_copy(ref, ref, sem).wait()
+
     def go(c):
         c.start()
 
     def sent(c):
         c.wait_send()
 
-    tail = jnp.logical_and(src_j == NB - 1, src_b < NB - 1)
-
-    def halo(a, o, act):
-        src, dst, _ = arrays[a]
-        hd = lax.rem(h + o, NB)
-        to = place(src_b + 1, hd)
-
-        def remote():
+    def halo(a, act):
+        dst = arrays[a][1]
+
+        @pl.when(b < NB - 1)
+        def _():
             act(pltpu.make_async_remote_copy(
-                src.at[hd, pl.ds(CH - WIN, WIN)], dst.at[pl.ds(0, WIN)], h_send.at[a], h_recv.at[a],
-                device_id=ctx(to), device_id_type=MESH))
-
-        if o == 0:
-            pl.when(to != me)(remote)
-            if act is go:
-                @pl.when(to == me)
-                def _():
-                    pltpu.make_async_copy(
-                        src.at[hd, pl.ds(CH - WIN, WIN)], dst.at[pl.ds(0, WIN)], h_recv.at[a]).start()
-        else:
-            remote()
+                dst.at[pl.ds(NB * CH, WIN)], dst.at[pl.ds(0, WIN)], h_send.at[a], h_recv.at[a],
+                device_id=ctx(place(b + 1, h)), device_id_type=MESH))
 
     for a in range(4):
         for o in FAR:
             exchange(a, o, go)
-        if a < 2:
-            @pl.when(tail)
-            def _():
-                for o in FAR:
-                    halo(a, o, go)
 
     @pl.when(first_block)
     def _():
         kbuf[pl.ds(0, WIN)] = jnp.zeros((WIN, HD), BF)
         vbuf[pl.ds(0, WIN)] = jnp.zeros((WIN, HD), BF)
 
+    ci = lax.broadcasted_iota(jnp.int32, (CH + WIN, CH), 0)
+    ii = lax.broadcasted_iota(jnp.int32, (CH + WIN, CH), 1)
+    inwin = jnp.logical_and(ci > ii, ci <= ii + WIN)
+    mask[0] = jnp.where(jnp.logical_and(inwin, jnp.logical_or(ci >= WIN, b > 0)), 0.0, -jnp.inf)
+    mask[1] = jnp.where(inwin, 0.0, -jnp.inf)
     eye = jnp.where(
         lax.broadcasted_iota(jnp.int32, (CH, CH), 0) == lax.broadcasted_iota(jnp.int32, (CH, CH), 1),
         1.0, 0.0).astype(BF)
@@ -200,22 +178,15 @@
         part = dst.at[pl.ds(base, NB * CH)]
         pltpu.make_async_copy(part, part, x_recv.at[a]).wait()
 
-    def halo_arrived(a):
-        dst = arrays[a][1]
-        part = dst.at[pl.ds(0, WIN)]
-        pltpu.make_async_copy(part, part, h_recv.at[a]).wait()
-
     arrived(0)
-
-    @pl.when(b > 0)
-    def _():
-        halo_arrived(0)
+    halo(0, go)
 
     cidx = lax.broadcasted_iota(jnp.int32, (CH, CH), 0)
     iidx = lax.broadcasted_iota(jnp.int32, (CH, CH), 1)
     lower = cidx <= iidx
 
-    sums = [jnp.zeros((AUG, CH), F32)]
+    def edges(buf):
+        return jnp.concatenate([buf[pl.ds(WIN, WIN)], buf[pl.ds(NB * CH, WIN)]], axis=0)
 
     def key_chunk(n):
         f = halves(nt(w2k, kbuf[pl.ds(n * CH, CH)]))
@@ -223,45 +194,55 @@
             bad = jnp.logical_and(first_block, iidx < WIN)
             f = jnp.where(bad, 0.0, f)
         fkt[n] = f
-        fb = f.astype(BF)
-        fk = nt(eye, fb).astype(BF)
-        fkb[n] = fk
-
-    each(key_chunk)
+        fkb[n] = nt(eye, f.astype(BF)).astype(BF)
+
+    for n in range(1, NB):
+        key_chunk(n)
+    fkx = nt(eye, halves(nt(w2k, edges(kbuf))).astype(BF)).astype(BF)
     arrived(1)
-
-    @pl.when(b > 0)
-    def _():
-        halo_arrived(1)
+    halo(1, go)
 
     def value_chunk(n):
         va = jnp.concatenate([nt(eye, vbuf[pl.ds(n * CH, CH)]), one_row], axis=0).astype(BF)
         vta[n] = va
-        pre[n] = sums[-1]
-        sums.append(sums[-1] + nn(va, fkb[n]))
-
-    each(value_chunk)
+        return nn(va, fkb[n])
+
+    vax = jnp.concatenate([nt(eye, edges(vbuf)), one_row], axis=0).astype(BF)
+    head_sum = nn(vax[:, :WIN], fkx[:WIN])
+    run = head_sum
+    for n in range(1, NB):
+        pre[n] = run
+        run = run + value_chunk(n)
+    own1[...] = split(run + nn(vax[:, WIN:], fkx[WIN:]))
     vta[NB, :, pl.ds(0, WIN)] = jnp.concatenate(
         [nt(eye, vbuf[pl.ds(NB * CH, WIN)]), one_row[:, :WIN]], axis=0).astype(BF)
-    own1[...] = split(sums[-1])
-
-    def scan_copy(o, own, got, send, recv):
+
+    def scan_copy(o, own, got, recv):
         return pltpu.make_async_remote_copy(
-            own, got.at[b], send.at[o], recv.at[b], device_id=ctx(place(lax.rem(b + o, NB), h)),
+            own, got.at[b], a_send, recv, device_id=ctx(place(lax.rem(b + o, NB), h)),
             device_id_type=MESH)
 
     def forward(o, act):
         @pl.when(b + o < NB)
         def _():
-            act(scan_copy(o, own1, ag1, a1_send, a1_recv))
+            act(scan_copy(o, own1, ag1, a1_recv))
 
     def backward(o, act):
         @pl.when(b - o >= 0)
         def _():
-            act(scan_copy(NB - o, own2, ag2, a2_send, a2_recv))
+            act(scan_copy(NB - o, own2, ag2, a2_recv))
 
     for o in range(7, 0, -1):
         forward(o, go)
+
+    @pl.when(b > 0)
+    def _():
+        for a in range(2):
+            part = arrays[a][1].at[pl.ds(0, WIN)]
+            pltpu.make_async_copy(part, part, h_recv.at[a]).wait()
+
+    key_chunk(0)
+    pre[0] = head_sum - value_chunk(0)
 
     arrived(2)
     scale = 1.0 / HD**0.5
@@ -273,12 +254,7 @@
         fb = f.astype(BF)
         fqb[n] = fb
         sc = nt(kbuf[pl.ds(n * CH, CH + WIN)], q) * scale
-        ci = lax.broadcasted_iota(jnp.int32, (CH + WIN, CH), 0)
-        ii = lax.broadcasted_iota(jnp.int32, (CH + WIN, CH), 1)
-        inwin = jnp.logical_and(ci > ii, ci <= ii + WIN)
-        if n == 0:
-            inwin = jnp.logical_and(inwin, jnp.logical_or(ci >= WIN, b > 0))
-        sc = jnp.where(inwin, sc, -jnp.inf)
+        sc = sc + mask[1 if n else 0]
         top = jnp.max(sc, axis=0, keepdims=True)
         w = jnp.exp(sc - top).astype(BF)
         wn = nn(vta[n], w[:CH]) + nn(vta[n + 1, :, pl.ds(0, WIN)], w[CH:])
@@ -296,10 +272,14 @@
     each(query_chunk)
 
     lin[...] = jnp.zeros((AUG, CH), F32)
+    for k in range(1, NB):
+        @pl.when(b == k)
+        def _():
+            left(ag1.at[pl.ds(0, k)], a1_recv)
+
     for m in range(NB - 1):
         @pl.when(m < b)
         def _():
-            pltpu.make_async_copy(ag1.at[m], ag1.at[m], a1_recv.at[m]).wait()
             lin[...] += ag1[m].astype(F32)
     carry = joined(lin[...])
     carry_b = split(carry)
@@ -340,17 +320,17 @@
 
     def loss_a(o, act):
         act(pltpu.make_async_remote_copy(
-            la.at[b], la.at[b], l_send.at[0], l_recv.at[0],
+            la.at[b], la.at[b], l_send, l_recv.at[0],
             device_id=ctx(place(lax.rem(b + o, NB), h)), device_id_type=MESH))
 
     def loss_b(o, act):
         act(pltpu.make_async_remote_copy(
-            lb.at[xme], lb.at[xme], l_send.at[1], l_recv.at[1],
+            lb.at[xme], lb.at[xme], l_send, l_recv.at[1],
             device_id={"head": lax.rem(xme + o, 4)}, device_id_type=MESH))
 
     def loss_c(o, act):
         act(pltpu.make_async_remote_copy(
-            lc.at[h], lc.at[h], l_send.at[2], l_recv.at[2],
+            lc.at[h], lc.at[h], l_send, l_recv.at[2],
             device_id=ctx(place(b, lax.rem(h + o, NB))), device_id_type=MESH))
 
     def total(ref, count, level):
@@ -396,14 +376,19 @@
         gfk[n] = nt(fqb[n], mx) + nn(lt, vta[n])
 
     each(mix_chunk)
-    gsum[0, b] = nn(jnp.concatenate(dq, axis=1), qbuf[...]).astype(BF)
+    gpart[0] = nn(jnp.concatenate(dq, axis=1), qbuf[...]).astype(BF)
+
+    def half(core):
+        return pl.ds(pl.multiple_of(HF // 2 * core, HF // 2), HF // 2)
 
     def share(w, o, act):
+        m = lax.rem(b + o, NB)
         act(pltpu.make_async_remote_copy(
-            gsum.at[w, b], gsum.at[w, b], r_send.at[w], r_recv.at[w],
-            device_id=ctx(place(lax.rem(b + o, NB), h)), device_id_type=MESH))
+            gpart.at[w, half(lax.rem(m, 2))], gsum.at[w, b], r_send, r_recv.at[w],
+            device_id=ctx(place(m, h)), device_id_type=MESH))
 
     def summed(w):
+        gsum[w, b] = gpart[w, half(c)]
         part = gsum.at[w, pl.ds(0, NB - 1)]
         pltpu.make_async_copy(part, part, r_recv.at[w]).wait()
         acc = gsum[w, 0].astype(F32)
@@ -413,13 +398,26 @@
 
     def spread(w, o, act):
         act(pltpu.make_async_remote_copy(
-            fin.at[w], fin_out.at[w, h], f_send.at[w], f_recv.at[w],
+            fin.at[w], fin_out.at[w, h, half(c)], f_send, f_recv.at[w, o],
             device_id=ctx(place(b, lax.rem(h + o, NB))), device_id_type=MESH))
+
+    def partner(w, src, head):
+        pltpu.make_async_remote_copy(
+            src, fin_out.at[w, head, half(c)], g_send, g_recv,
+            device_id=ctx(me + 1 - 2 * c), device_id_type=MESH).start()
 
     def spread_all(w):
         for o in FAR[:-1]:
             spread(w, o, go)
-        pltpu.make_async_copy(fin.at[w], fin_out.at[w, h], f_recv.at[w]).start()
+        pltpu.make_async_copy(fin.at[w], fin_out.at[w, h, half(c)], f_recv.at[w, 0]).start()
+        partner(w, fin.at[w], h)
+
+    def pass_on(w):
+        for o in reversed(FAR[:-1]):
+            head = lax.rem(h - o + NB, NB)
+            mine = fin_out.at[w, head, half(c)]
+            pltpu.make_async_copy(mine, mine, f_recv.at[w, o]).wait()
+            partner(w, mine, head)
 
     for o in range(1, NB):
         share(0, o, go)
@@ -428,10 +426,14 @@
         loss_b(o, go)
 
     lin[...] = jnp.zeros((AUG, CH), F32)
+    for k in range(1, NB):
+        @pl.when(b == NB - 1 - k)
+        def _():
+            left(ag2.at[pl.ds(NB - k, k)], a2_recv)
+
     for m in range(1, NB):
         @pl.when(m > b)
         def _():
-            pltpu.make_async_copy(ag2.at[m], ag2.at[m], a2_recv.at[m]).wait()
             lin[...] += ag2[m].astype(F32)
     after = nt(eye, split(joined(lin[...]))).astype(BF)
     dk = []
@@ -440,54 +442,46 @@
         dk.append(proj_grad(fkt[n], gfk[n] + nn(after, vta[n])))
 
     each(key_grad)
-    gsum[1, b] = nn(jnp.concatenate(dk, axis=1), kbuf[pl.ds(0, NB * CH)]).astype(BF)
+    gpart[1] = nn(jnp.concatenate(dk, axis=1), kbuf[pl.ds(0, NB * CH)]).astype(BF)
     for o in range(1, NB):
         share(1, o, go)
     summed(0)
     spread_all(0)
-    summed(1)
-    spread_all(1)
-
     lc[h] = total(lb, 4, 1)
     for o in range(1, NB):
         loss_c(o, go)
+    summed(1)
+    spread_all(1)
+
     pltpu.make_async_copy(stu_got, stu_got, s_recv).wait()
     stu_t[...] = jnp.swapaxes(stu_got[...], 0, 1)
     put = pltpu.make_async_copy(stu_t, stu_out, out_sem)
     put.start()
-
-    def left(ref, sem):
-        pltpu.make_async_copy(ref, ref, sem).wait()
+    pass_on(0)
+    pass_on(1)
 
     own = (me == place(src_b, h)).astype(jnp.int32)
     for n in range(2):
         @pl.when(own == n)
         def _():
-            for a in range(4):
-                left(qbuf.at[pl.ds(0, CH * (NB - n))], x_send.at[a])
+            left(xs.at[:, pl.ds(0, NB - n)], x_send)
             left(stu.at[pl.ds(0, NB - n)], s_send)
 
-        @pl.when(jnp.logical_and(tail, (me == place(src_b + 1, h)).astype(jnp.int32) == n))
-        def _():
-            for a in range(2):
-                left(qbuf.at[pl.ds(0, WIN * (NB - n))], h_send.at[a])
-
-    for o in range(1, NB):
-        forward(o, sent)
-        backward(o, sent)
-    left(la.at[pl.ds(0, NB - 1)], l_send.at[0])
-    left(lb.at[pl.ds(0, 3)], l_send.at[1])
-    left(lc.at[pl.ds(0, NB - 1)], l_send.at[2])
-    for w in range(2):
-        left(gsum.at[w, pl.ds(0, NB - 1)], r_send.at[w])
-        left(gsum.at[w, pl.ds(0, NB - 1)], f_send.at[w])
+    for a in range(2):
+        halo(a, sent)
+    left(ag1.at[pl.ds(0, NB - 1)], a_send)
+    left(win.at[0, pl.ds(0, 8 * 17)], l_send)
+    left(gsum.at[:, pl.ds(0, NB - 1)], r_send)
+    left(gsum.at[:, pl.ds(0, NB - 1)], f_send)
     loss[...] = jnp.sum(total(lc, NB, 2), keepdims=True) * (1.0 / (8192 * 32 * 128))
     put_loss = pltpu.make_async_copy(loss, loss_out, loss_sem)
     put_loss.start()
     put.wait()
     put_loss.wait()
     for w in range(2):
-        pltpu.make_async_copy(fin_out.at[w], fin_out.at[w], f_recv.at[w]).wait()
+        left(fin.at[w], f_recv.at[w, 0])
+    left(gsum, g_send)
+    left(gsum, g_recv)
 
 
 def finish(stu_in, fin_in, loss_in, stu_out, gq_out, gk_out, loss_out, fin, gq, gk, loss, in_sem, out_sem):
@@ -553,22 +547,24 @@
             pltpu.VMEM((NB, CH, HD), BF),
             pltpu.VMEM((NB, CH, HD), BF),
             pltpu.VMEM((CH, NB, HD), BF),
-            pltpu.VMEM((2, NB, HF, HD), BF),
             pltpu.VMEM((2, HF, HD), BF),
+            pltpu.VMEM((2, NB, HF // 2, HD), BF),
+            pltpu.VMEM((2, HF // 2, HD), BF),
             pltpu.VMEM((NB, 8, CH), F32),
             pltpu.VMEM((4, 8, CH), F32),
             pltpu.VMEM((NB, 8, CH), F32),
             pltpu.VMEM((1, 1), F32),
             pltpu.VMEM((NB, 8, CH), F32),
+            pltpu.VMEM((2, CH + WIN, CH), F32),
             dma((4,)), dma((2,)), dma, dma,
-            dma((4,)), dma((4,)),
+            dma, dma((4,)),
             dma((2,)), dma((2,)),
-            dma((NB,)), dma((NB,)),
-            dma((NB,)), dma((NB,)),
+            dma, dma, dma,
             dma, dma,
-            dma((2,)), dma((2,)),
-            dma((2,)), dma((2,)),
-            dma((3,)), dma((3,)),
+            dma, dma((2,)),
+            dma, dma((2, NB)),
+            dma, dma,
+            dma, dma((3,)),
         ],
         compiler_params=pltpu.CompilerParams(
             collective_id=0, has_side_effects=True, vmem_limit_bytes=24 * 2**20),

time: 57.1 us -> 54.3 us (0.951)
  Pallas kernels: 56.3 us -> 53.6 us
    pallas_call x1, Pallas kernels: 54.8 us -> 52 us  [per_device(): pl.pallas_call(kernel, out_shape=(jax.ShapeDtypeStruct((CH, NB, HD), BF),...]
where the time goes in v4:
time: 54.3 us; the launch traced here: 54.2 us
  Pallas kernels  53.6 us (99%)
  between operations  0.64 us (1%)
    pallas_call x1, Pallas kernels, per_device(): pl.pallas_call(kernel, out_shape=(jax.ShapeDtypeStruct((CH, NB, HD), BF),...  52 us
    pallas_call x1, Pallas kernels, per_device(): pl.pallas_call(finish, out_shape=(jax.ShapeDtypeStruct((CH, NB, HD), BF),...  1.58 us

profile of v4, /device:TPU:1, one launch (start us, length us, event | category | flops | bytes accessed | tf_op | source)
XLA Modules:
  0.0 54.2 jit_solution(15672630043810027145)
XLA Ops:
  0.6 52.0 %shard_map.93 = (bf16[128,8,128]{2,1,0:T(8,128)(2,1)S(1)}, bf16[2,8,64,128]{3,2,1,0:T(8,128)(2,1)S(1)}, f32[1,1]{1,0:T(1,128)}) custom-call(bf16[128,8,128]{2,1,0:T(8,128)(2,1)} %q_hbm.1, bf16[128,8,128]{2,1,0:T(8,128)(2,1)} %k_hbm.1, bf16[128,8,128]{2,1,0:T(8,128)(2,1)} %v_hbm.1, bf16[128,8,128]{2,1,0:T(8,128)(2,1)} %t_hbm.1, bf16[8,64,128]{2,1,0:T(8,128)(2,1)} %wq_hbm.1, ...), custom_call_target="tpu_custom_call" | custom-call | tf_op jit(solution)/shard_map/pallas_call | solution.py:513
  52.6 1.6 %shard_map.94 = (bf16[128,8,128]{2,1,0:T(8,128)(2,1)}, f32[8,64,128]{2,1,0:T(8,128)}, f32[8,64,128]{2,1,0:T(8,128)}, f32[1,1]{1,0:T(1,128)}) custom-call(bf16[128,8,128]{2,1,0:T(8,128)(2,1)S(1)} %get-tuple-element.11.stu_in, bf16[2,8,64,128]{3,2,1,0:T(8,128)(2,1)S(1)} %get-tuple-element.12.fin_in, f32[1,1]{1,0:T(1,128)} %get-tuple-element.13.loss_in), custom_call_target="tpu_custom_call" | custom-call | tf_op jit(solution)/shard_map/pallas_call | solution.py:572

commit v5 on v4

--- a/solution.py
+++ b/solution.py
@@ -66,9 +66,9 @@
     q_hbm, k_hbm, v_hbm, t_hbm, wq_hbm, wk_hbm,
     stu_out, fin_out, loss_out,
     xin, xs, wq_ref, wk_ref,
-    kbuf, vbuf, qbuf, tbuf, fkt, fkb, fqt, fqb, vta, pre, win, outs, lin, gna, gfk, later,
-    own1, ag1, own2, ag2, stu, stu_got, stu_t, gpart, gsum, fin, la, lb, lc, loss, scal, mask,
-    in_sem, w_sem, out_sem, loss_sem,
+    kbuf, vbuf, qbuf, tbuf, fkt, fkb, fqt, fqb, vta, pre, win, outs, diffs, lin, gna, gfk, later,
+    own1, ag1, own2, ag2, stu, stu_got, stu_t, gpart, gsum, fin, la, lb, lc, scal, mask,
+    in_sem, w_sem, out_sem,
     x_send, x_recv, h_send, h_recv, a_send, a1_recv, a2_recv,
     s_send, s_recv, r_send, r_recv, f_send, f_recv, g_send, g_recv, l_send, l_recv,
 ):
@@ -293,18 +293,16 @@
 
     each(out_chunk)
     arrived(3)
-    errors, suffix = [], [jnp.zeros((AUG, CH), F32)]
+    suffix = [jnp.zeros((AUG, CH), F32)]
 
     def diff_chunk(k):
         n = NB - 1 - k
         coef, out = scal[n][:1], outs[n]
         diff = out - nt(eye, tbuf[pl.ds(n * CH, CH)])
-        sq = diff * diff
-        for r in range(HD // 8):
-            errors.append(sq[8 * r : 8 * r + 8])
         g = diff * (2.0 / HD)
         gd = -coef * jnp.sum(g * out, axis=0, keepdims=True)
         scal[n] = jnp.broadcast_to(gd, (8, CH))
+        diffs[n] = diff
         ga = jnp.concatenate([coef * g, gd * one_row], axis=0).astype(BF)
         gna[n] = ga
         later[n] = suffix[-1]
@@ -312,11 +310,16 @@
 
     each(diff_chunk)
     own2[...] = split(suffix[-1])
+    for o in range(7, 0, -1):
+        backward(o, go)
+    errors = []
+    for n in range(NB):
+        sq = diffs[n] * diffs[n]
+        for r in range(HD // 8):
+            errors.append(sq[8 * r : 8 * r + 8])
     while len(errors) > 1:
         errors = [sum(errors[i : i + 2]) for i in range(0, len(errors), 2)]
     la[b] = errors[0]
-    for o in range(7, 0, -1):
-        backward(o, go)
 
     def loss_a(o, act):
         act(pltpu.make_async_remote_copy(
@@ -330,7 +333,7 @@
 
     def loss_c(o, act):
         act(pltpu.make_async_remote_copy(
-            lc.at[h], lc.at[h], l_send, l_recv.at[2],
+            lc, loss_out.at[h], l_send, l_recv.at[2],
             device_id=ctx(place(b, lax.rem(h + o, NB))), device_id_type=MESH))
 
     def total(ref, count, level):
@@ -447,11 +450,12 @@
         share(1, o, go)
     summed(0)
     spread_all(0)
-    lc[h] = total(lb, 4, 1)
+    summed(1)
+    spread_all(1)
+    lc[...] = total(lb, 4, 1)
     for o in range(1, NB):
         loss_c(o, go)
-    summed(1)
-    spread_all(1)
+    pltpu.make_async_copy(lc, loss_out.at[h], l_recv.at[2]).start()
 
     pltpu.make_async_copy(stu_got, stu_got, s_recv).wait()
     stu_t[...] = jnp.swapaxes(stu_got[...], 0, 1)
@@ -473,21 +477,18 @@
     left(win.at[0, pl.ds(0, 8 * 17)], l_send)
     left(gsum.at[:, pl.ds(0, NB - 1)], r_send)
     left(gsum.at[:, pl.ds(0, NB - 1)], f_send)
-    loss[...] = jnp.sum(total(lc, NB, 2), keepdims=True) * (1.0 / (8192 * 32 * 128))
-    put_loss = pltpu.make_async_copy(loss, loss_out, loss_sem)
-    put_loss.start()
     put.wait()
-    put_loss.wait()
+    left(loss_out, l_recv.at[2])
     for w in range(2):
         left(fin.at[w], f_recv.at[w, 0])
     left(gsum, g_send)
     left(gsum, g_recv)
 
 
-def finish(stu_in, fin_in, loss_in, stu_out, gq_out, gk_out, loss_out, fin, gq, gk, loss, in_sem, out_sem):
+def finish(stu_in, fin_in, loss_in, stu_out, gq_out, gk_out, loss_out, fin, gq, gk, parts, loss, in_sem, out_sem):
     loads = [
         pltpu.make_async_copy(src, dst, in_sem.at[i])
-        for i, (src, dst) in enumerate(((fin_in, fin), (loss_in, loss)))
+        for i, (src, dst) in enumerate(((fin_in.at[0], fin.at[0]), (fin_in.at[1], fin.at[1]), (loss_in, parts)))
     ]
     stores = [
         pltpu.make_async_copy(src, dst, out_sem.at[i])
@@ -499,9 +500,11 @@
     loads[0].wait()
     gq[...] = fin[0].astype(F32)
     stores[0].start()
+    loads[1].wait()
     gk[...] = fin[1].astype(F32)
     stores[1].start()
-    loads[1].wait()
+    loads[2].wait()
+    loss[...] = jnp.sum(parts[...], keepdims=True)[0] * (1.0 / (8192 * 32 * 128))
     stores[2].start()
     for store in stores:
         store.wait()
@@ -515,7 +518,7 @@
         out_shape=(
             jax.ShapeDtypeStruct((CH, NB, HD), BF),
             jax.ShapeDtypeStruct((2, NB, HF, HD), BF),
-            jax.ShapeDtypeStruct((1, 1), F32),
+            jax.ShapeDtypeStruct((NB, 8, CH), F32),
         ),
         in_specs=[anywhere] * 6,
         out_specs=(anywhere,) * 3,
@@ -536,6 +539,7 @@
             pltpu.VMEM((NB, AUG, CH), F32),
             pltpu.VMEM((NB, AUG, CH), F32),
             pltpu.VMEM((NB, HD, CH), F32),
+            pltpu.VMEM((NB, HD, CH), F32),
             pltpu.VMEM((AUG, CH), F32),
             pltpu.VMEM((NB, AUG, CH), BF),
             pltpu.VMEM((NB, CH, CH), F32),
@@ -552,11 +556,10 @@
             pltpu.VMEM((2, HF // 2, HD), BF),
             pltpu.VMEM((NB, 8, CH), F32),
             pltpu.VMEM((4, 8, CH), F32),
-            pltpu.VMEM((NB, 8, CH), F32),
-            pltpu.VMEM((1, 1), F32),
+            pltpu.VMEM((8, CH), F32),
             pltpu.VMEM((NB, 8, CH), F32),
             pltpu.VMEM((2, CH + WIN, CH), F32),
-            dma((4,)), dma((2,)), dma, dma,
+            dma((4,)), dma((2,)), dma,
             dma, dma((4,)),
             dma((2,)), dma((2,)),
             dma, dma, dma,
@@ -583,8 +586,9 @@
             pltpu.VMEM((2, NB, HF, HD), BF),
             pltpu.VMEM((NB, HF, HD), F32),
             pltpu.VMEM((NB, HF, HD), F32),
+            pltpu.VMEM((NB, 8, CH), F32),
             pltpu.VMEM((1, 1), F32),
-            dma((2,)),
+            dma((3,)),
             dma((4,)),
         ],
         compiler_params=pltpu.CompilerParams(vmem_limit_bytes=8 * 2**20),

time: 54.3 us -> 53.4 us (0.983)
  Pallas kernels: 53.6 us -> 52.7 us
    pallas_call x1, Pallas kernels: 52 us -> 51.3 us  [per_device(): pl.pallas_call(kernel, out_shape=(jax.ShapeDtypeStruct((CH, NB, HD), BF),...]
where the time goes in v5:
time: 53.4 us; the launch traced here: 53.3 us
  Pallas kernels  52.7 us (99%)
  between operations  0.64 us (1%)
    pallas_call x1, Pallas kernels, per_device(): pl.pallas_call(kernel, out_shape=(jax.ShapeDtypeStruct((CH, NB, HD), BF),...  51.3 us
    pallas_call x1, Pallas kernels, per_device(): pl.pallas_call(finish, out_shape=(jax.ShapeDtypeStruct((CH, NB, HD), BF),...  1.32 us

profile of v5, /device:TPU:1, one launch (start us, length us, event | category | flops | bytes accessed | tf_op | source)
XLA Modules:
  0.0 53.3 jit_solution(17359423184320102850)
XLA Ops:
  0.6 51.3 %shard_map.93 = (bf16[128,8,128]{2,1,0:T(8,128)(2,1)S(1)}, bf16[2,8,64,128]{3,2,1,0:T(8,128)(2,1)S(1)}, f32[8,8,128]{2,1,0:T(8,128)S(1)}) custom-call(bf16[128,8,128]{2,1,0:T(8,128)(2,1)} %q_hbm.1, bf16[128,8,128]{2,1,0:T(8,128)(2,1)} %k_hbm.1, bf16[128,8,128]{2,1,0:T(8,128)(2,1)} %v_hbm.1, bf16[128,8,128]{2,1,0:T(8,128)(2,1)} %t_hbm.1, ...), custom_call_target="tpu_custom_call" | custom-call | tf_op jit(solution)/shard_map/pallas_call | solution.py:516
  52.0 1.3 %shard_map.94 = (bf16[128,8,128]{2,1,0:T(8,128)(2,1)}, f32[8,64,128]{2,1,0:T(8,128)}, f32[8,64,128]{2,1,0:T(8,128)}, f32[1,1]{1,0:T(1,128)}) custom-call(bf16[128,8,128]{2,1,0:T(8,128)(2,1)S(1)} %get-tuple-element.11.stu_in, bf16[2,8,64,128]{3,2,1,0:T(8,128)(2,1)S(1)} %get-tuple-element.12.fin_in, f32[8,8,128]{2,1,0:T(8,128)S(1)} %get-tuple-element.13.loss_in), custom_call_target="tpu_custom_call" | custom-call | tf_op jit(solution)/shard_map/pallas_call | solution.py:575

commit v6 on v5

--- a/solution.py
+++ b/solution.py
@@ -293,10 +293,9 @@
 
     each(out_chunk)
     arrived(3)
-    suffix = [jnp.zeros((AUG, CH), F32)]
-
-    def diff_chunk(k):
-        n = NB - 1 - k
+    parts = []
+
+    def diff_chunk(n):
         coef, out = scal[n][:1], outs[n]
         diff = out - nt(eye, tbuf[pl.ds(n * CH, CH)])
         g = diff * (2.0 / HD)
@@ -305,11 +304,11 @@
         diffs[n] = diff
         ga = jnp.concatenate([coef * g, gd * one_row], axis=0).astype(BF)
         gna[n] = ga
-        later[n] = suffix[-1]
-        suffix.append(suffix[-1] + nt(ga, fqb[n]))
+        parts.append(ga)
 
     each(diff_chunk)
-    own2[...] = split(suffix[-1])
+    queries_all = jnp.concatenate([fqb[n] for n in range(NB)], axis=1)
+    own2[...] = split(nt(jnp.concatenate(parts, axis=1), queries_all))
     for o in range(7, 0, -1):
         backward(o, go)
     errors = []
@@ -378,6 +377,10 @@
         lt = nt(eye, split(later[n])).astype(BF)
         gfk[n] = nt(fqb[n], mx) + nn(lt, vta[n])
 
+    suffix = jnp.zeros((AUG, CH), F32)
+    for n in reversed(range(NB)):
+        later[n] = suffix
+        suffix = suffix + nt(gna[n], fqb[n])
     each(mix_chunk)
     gpart[0] = nn(jnp.concatenate(dq, axis=1), qbuf[...]).astype(BF)
 

time: 53.4 us -> 53 us (level)
  no operation moved by 1% of the time
where the time goes in v6:
time: 53 us; the launch traced here: 52.9 us
  Pallas kernels  52.3 us (99%)
  between operations  0.64 us (1%)
    pallas_call x1, Pallas kernels, per_device(): pl.pallas_call(kernel, out_shape=(jax.ShapeDtypeStruct((CH, NB, HD), BF),...  51 us
    pallas_call x1, Pallas kernels, per_device(): pl.pallas_call(finish, out_shape=(jax.ShapeDtypeStruct((CH, NB, HD), BF),...  1.32 us

profile of v6, /device:TPU:1, one launch (start us, length us, event | category | flops | bytes accessed | tf_op | source)
XLA Modules:
  0.0 52.9 jit_solution(4355135478800724751)
XLA Ops:
  0.6 51.0 %shard_map.93 = (bf16[128,8,128]{2,1,0:T(8,128)(2,1)S(1)}, bf16[2,8,64,128]{3,2,1,0:T(8,128)(2,1)S(1)}, f32[8,8,128]{2,1,0:T(8,128)S(1)}) custom-call(bf16[128,8,128]{2,1,0:T(8,128)(2,1)} %q_hbm.1, bf16[128,8,128]{2,1,0:T(8,128)(2,1)} %k_hbm.1, bf16[128,8,128]{2,1,0:T(8,128)(2,1)} %v_hbm.1, bf16[128,8,128]{2,1,0:T(8,128)(2,1)} %t_hbm.1, ...), custom_call_target="tpu_custom_call" | custom-call | tf_op jit(solution)/shard_map/pallas_call | solution.py:519
  51.6 1.3 %shard_map.94 = (bf16[128,8,128]{2,1,0:T(8,128)(2,1)}, f32[8,64,128]{2,1,0:T(8,128)}, f32[8,64,128]{2,1,0:T(8,128)}, f32[1,1]{1,0:T(1,128)}) custom-call(bf16[128,8,128]{2,1,0:T(8,128)(2,1)S(1)} %get-tuple-element.11.stu_in, bf16[2,8,64,128]{3,2,1,0:T(8,128)(2,1)S(1)} %get-tuple-element.12.fin_in, f32[8,8,128]{2,1,0:T(8,128)S(1)} %get-tuple-element.13.loss_in), custom_call_target="tpu_custom_call" | custom-call | tf_op jit(solution)/shard_map/pallas_call | solution.py:578

commit v7 on v6

--- a/solution.py
+++ b/solution.py
@@ -309,7 +309,7 @@
     each(diff_chunk)
     queries_all = jnp.concatenate([fqb[n] for n in range(NB)], axis=1)
     own2[...] = split(nt(jnp.concatenate(parts, axis=1), queries_all))
-    for o in range(7, 0, -1):
+    for o in range(1, NB):
         backward(o, go)
     errors = []
     for n in range(NB):

time: 53 us -> 53 us (level)
  no operation moved by 1% of the time
where the time goes in v7:
time: 53 us; the launch traced here: 52.9 us
  Pallas kernels  52.3 us (99%)
  between operations  0.64 us (1%)
    pallas_call x1, Pallas kernels, per_device(): pl.pallas_call(kernel, out_shape=(jax.ShapeDtypeStruct((CH, NB, HD), BF),...  51 us
    pallas_call x1, Pallas kernels, per_device(): pl.pallas_call(finish, out_shape=(jax.ShapeDtypeStruct((CH, NB, HD), BF),...  1.32 us

profile of v7, /device:TPU:1, one launch (start us, length us, event | category | flops | bytes accessed | tf_op | source)
XLA Modules:
  0.0 52.9 jit_solution(14516837332813859901)
XLA Ops:
  0.6 51.0 %shard_map.93 = (bf16[128,8,128]{2,1,0:T(8,128)(2,1)S(1)}, bf16[2,8,64,128]{3,2,1,0:T(8,128)(2,1)S(1)}, f32[8,8,128]{2,1,0:T(8,128)S(1)}) custom-call(bf16[128,8,128]{2,1,0:T(8,128)(2,1)} %q_hbm.1, bf16[128,8,128]{2,1,0:T(8,128)(2,1)} %k_hbm.1, bf16[128,8,128]{2,1,0:T(8,128)(2,1)} %v_hbm.1, bf16[128,8,128]{2,1,0:T(8,128)(2,1)} %t_hbm.1, ...), custom_call_target="tpu_custom_call" | custom-call | tf_op jit(solution)/shard_map/pallas_call | solution.py:519
  51.6 1.3 %shard_map.94 = (bf16[128,8,128]{2,1,0:T(8,128)(2,1)}, f32[8,64,128]{2,1,0:T(8,128)}, f32[8,64,128]{2,1,0:T(8,128)}, f32[1,1]{1,0:T(1,128)}) custom-call(bf16[128,8,128]{2,1,0:T(8,128)(2,1)S(1)} %get-tuple-element.11.stu_in, bf16[2,8,64,128]{3,2,1,0:T(8,128)(2,1)S(1)} %get-tuple-element.12.fin_in, f32[8,8,128]{2,1,0:T(8,128)S(1)} %get-tuple-element.13.loss_in), custom_call_target="tpu_custom_call" | custom-call | tf_op jit(solution)/shard_map/pallas_call | solution.py:578
